TPU v7x, 32 devices: a whole 2x2x4 slice. The times are simulated.
32 devices in a mesh: expert: 8 (over y, x, core), blk: 4 (over z).
Axes of the slice: x: 2, y: 2, z: 4, core: 2. Of those that a mesh axis runs over, the one named last changes fastest.
Arguments:
- tokens: bfloat16 [256, 6144], P(('expert', 'blk')), may hold values from -6 to 6
- out_grad: bfloat16 [256, 6144], P(('expert', 'blk')), may hold values from -6 to 6
- expert_ids: int32 [256, 4], P(('expert', 'blk')), may hold values from 0 to 7, as said below
- slots: int32 [256, 4], P(('expert', 'blk')), may hold values from 0 to 4, as said below
- gates: bfloat16 [256, 4], P(('expert', 'blk')), may hold values from 0.099609375 to 0.59765625
- w_in: bfloat16 [8, 5376, 6144], P('expert', 'blk'), may hold values from -0.078125 to 0.078125
- w_down: bfloat16 [8, 5376, 6144], P('expert', 'blk'), may hold values from -0.078125 to 0.078125
Outputs:
- grad_tokens: bfloat16 [256, 6144], P(('expert', 'blk'))
- grad_gates: bfloat16 [256, 4], P(('expert', 'blk'))
Inputs may be any that keep to these rules, and one draw needn't show every extreme that they name: `expert_ids`: within the 8 tokens of one device, a token names 4 different experts, no expert is named more than 5 times, and one expert is named exactly 5 times by every device. Among the entries of one device that name one expert, the slots are 0 to their count minus 1, each once.
All inputs are finite; a program needn't handle non-finite values.
Results may differ from a plain program's by a relative error of at most 0.019.
Values may be sent and summed in bfloat16 or wider, within the bound.
No kernel may reach another device: no remote copies, remote signals or barrier semaphores. Data moves between devices by JAX's collectives and lax.ppermute only.
A program may use at most 128 MiB of HBM per device.

v0:
```python
import jax
import jax.numpy as jnp
from jax import lax
from jax.sharding import PartitionSpec as P


def hidden_terms(rows_x, rows_dy, rows_gate, weight_in, weight_down):
    contract = (((1,), (1,)), ((), ()))
    pre = lax.dot_general(rows_x, weight_in, contract, preferred_element_type=jnp.float32)
    back = lax.dot_general(rows_dy, weight_down, contract, preferred_element_type=jnp.float32)
    sigma = jax.nn.sigmoid(pre)
    gate_part = jnp.sum(pre * sigma * back, axis=1)
    slope = rows_gate.astype(jnp.float32)[:, None] * back * sigma * (1.0 + pre * (1.0 - sigma))
    return (slope.astype(jnp.bfloat16), gate_part)


def per_device(tokens, out_grad, expert_ids, slots, gates, w_in, w_down):
    tok_count = tokens.shape[0]
    top_count = expert_ids.shape[1]
    expert_count = lax.axis_size("expert")
    capacity = max(2, (tok_count * top_count + expert_count - 1) // expert_count + 1)
    slot_count = expert_count * capacity
    target = expert_ids * capacity + slots
    matches = (target[None, :, :] == jnp.arange(slot_count, dtype=jnp.int32)[:, None, None]).astype(
        jnp.float32
    )
    placing = jnp.sum(matches, axis=2).astype(jnp.bfloat16)
    send_x = jnp.dot(placing, tokens, preferred_element_type=jnp.float32).astype(jnp.bfloat16)
    send_dy = jnp.dot(placing, out_grad, preferred_element_type=jnp.float32).astype(jnp.bfloat16)
    send_gate = jnp.einsum("stk,tk->s", matches, gates.astype(jnp.float32)).astype(jnp.bfloat16)
    recv_x, recv_dy, recv_gate = (
        lax.all_to_all(send_x, "expert", split_axis=0, concat_axis=0, tiled=True),
        lax.all_to_all(send_dy, "expert", split_axis=0, concat_axis=0, tiled=True),
        lax.all_to_all(send_gate, "expert", split_axis=0, concat_axis=0, tiled=True),
    )
    weight_in = w_in[0]
    weight_down = w_down[0]
    piece_slope, piece_gate = hidden_terms(
        lax.all_gather(recv_x, "blk", axis=0, tiled=True),
        lax.all_gather(recv_dy, "blk", axis=0, tiled=True),
        lax.all_gather(recv_gate, "blk", axis=0, tiled=True),
        weight_in,
        weight_down,
    )
    grad_rows = lax.psum_scatter(
        jnp.dot(piece_slope, weight_in, preferred_element_type=jnp.float32).astype(jnp.bfloat16),
        "blk",
        scatter_dimension=0,
        tiled=True,
    )
    gate_rows = lax.psum_scatter(piece_gate, "blk", scatter_dimension=0, tiled=True)
    back_rows, back_gate = (
        lax.all_to_all(grad_rows, "expert", split_axis=0, concat_axis=0, tiled=True),
        lax.all_to_all(
            gate_rows.astype(jnp.bfloat16), "expert", split_axis=0, concat_axis=0, tiled=True
        ),
    )
    grad_tokens = lax.dot_general(
        placing, back_rows, (((0,), (0,)), ((), ())), preferred_element_type=jnp.float32
    ).astype(jnp.bfloat16)
    grad_gates = jnp.einsum("stk,s->tk", matches, back_gate.astype(jnp.float32)).astype(
        jnp.bfloat16
    )
    return (grad_tokens, grad_gates)


def solution(mesh):
    return jax.shard_map(
        per_device,
        mesh=mesh,
        in_specs=(
            P(("expert", "blk"), None),
            P(("expert", "blk"), None),
            P(("expert", "blk"), None),
            P(("expert", "blk"), None),
            P(("expert", "blk"), None),
            P("expert", "blk", None),
            P("expert", "blk", None),
        ),
        out_specs=(P(("expert", "blk"), None), P(("expert", "blk"), None)),
        check_vma=False,
    )
```

profile of v0, /device:TPU:0, one launch (start us, length us, event | category | flops | bytes accessed | tf_op | source)
XLA Modules:
  0.0 203.6 jit_solution(10665111670085031153)
XLA Ops:
  7.2 0.7 multiply_add_fusion
  8.6 17.5 %all_to_all.62 = bf16[8,5,6144]{2,1,0:T(8,128)(2,1)S(1)} all-to-all(bf16[8,5,6144]{2,1,0:T(8,128)(2,1)S(1)} %all_to_all.46), channel_id=1, replica_groups=mesh['expert'=8,'blk'=4] {'expert'}, dimensions={0} | all-to-all | bytes 983040 | tf_op jit(solution)/shard_map/all_to_all | solution.py:32
  26.1 1.0 all_to_all.48
  27.2 1.2 convolution_convert_fusion.1
  28.7 14.9 %all_to_all.63 = bf16[8,5,6144]{2,1,0:T(8,128)(2,1)S(1)} all-to-all(bf16[8,5,6144]{2,1,0:T(8,128)(2,1)S(1)} %all_to_all.43), channel_id=1, replica_groups=mesh['expert'=8,'blk'=4] {'expert'}, dimensions={0} | all-to-all | bytes 983040 | tf_op jit(solution)/shard_map/all_to_all | solution.py:33
  43.6 1.0 all_to_all.45
  44.6 0.9 fusion.9
  45.5 0.7 all_to_all.55
  46.2 3.3 %all-to-all-start = ((bf16[8,5,1]{1,2,0:T(2,128)(2,1)}), bf16[8,5,1]{1,2,0:T(2,128)(2,1)S(1)}, u32[]{:S(2)}, u32[]{:S(2)}) async-start(bf16[8,5,1]{1,2,0:T(2,128)(2,1)} %all_to_all.55), calls=%async_computation | async-start | bytes 8192 | tf_op jit(solution)/shard_map/all_to_all | solution.py:34
  49.6 1.3 fusion.20
  51.4 2.6 %all-to-all-done = bf16[8,5,1]{1,2,0:T(2,128)(2,1)S(1)} async-done(((bf16[8,5,1]{1,2,0:T(2,128)(2,1)}), bf16[8,5,1]{1,2,0:T(2,128)(2,1)S(1)}, u32[]{:S(2)}, u32[]{:S(2)}) %all-to-all-start) | async-done | bytes 112 | tf_op jit(solution)/shard_map/all_to_all | solution.py:34
  54.4 12.8 %all-reduce = bf16[160]{0:T(256)(128)(2,1)S(1)} all-reduce(bf16[160]{0:T(256)(128)(2,1)S(1)} %dynamic-update-slice), channel_id=1, replica_groups=mesh['expert'=8,'blk'=4] {'blk'}, use_global_device_ids=true, to_apply=%add | all-reduce | flops 160 | bytes 640
  67.2 3.2 %all-gather.5.cloned.1.call-done = bf16[160,6144]{1,0:T(8,128)(2,1)} async-done(((bf16[40,6144]{1,0:T(8,128)(2,1)}), bf16[160,6144]{1,0:T(8,128)(2,1)}) %all-gather.5.cloned.1.call-update) | async-done | bytes 1966096 | tf_op jit(solution)/shard_map/all_gather | solution.py:39
  70.4 12.1 %fusion.2 = f32[160,1344]{1,0:T(8,128)S(1)} fusion(bf16[160,6144]{1,0:T(8,128)(2,1)} %all-gather.5.cloned.1.call-done, bf16[1,1344,6144]{2,1,0:T(8,128)(2,1)} %param.12), kind=kOutput, calls=%fused_computation.2 | convolution fusion | flops 2642411520 | bytes 19341312 | tf_op jit(solution)/shard_map/dot_general | solution.py:9
  82.5 31.9 %all-gather.3.cloned.1.call-done = bf16[160,6144]{1,0:T(8,128)(2,1)} async-done(((bf16[40,6144]{1,0:T(8,128)(2,1)}), bf16[160,6144]{1,0:T(8,128)(2,1)}) %all-gather.3.cloned.1.call-update) | async-done | bytes 1966096 | tf_op jit(solution)/shard_map/all_gather | solution.py:40
  114.4 12.2 %multiply_reduce_fusion = (f32[160]{0:T(256)S(1)}, f32[160,1344]{1,0:T(8,128)S(1)}) fusion(f32[160,1344]{1,0:T(8,128)S(1)} %fusion.2, bf16[160,6144]{1,0:T(8,128)(2,1)} %all-gather.3.cloned.1.call-done, bf16[1,1344,6144]{2,1,0:T(8,128)(2,1)} %param.13), kind=kOutput, calls=%fused_computation.12 | convolution fusion | flops 2643701504 | bytes 20202112 | tf_op jit(solution)/shard_map/dot_general | solution.py:10
  126.6 10.5 %fusion.6 = bf16[160,6144]{1,0:T(8,128)(2,1)} fusion(bf16[1,1344,6144]{2,1,0:T(8,128)(2,1)} %param.12, f32[160,1344]{1,0:T(8,128)S(1)} %fusion.2, f32[160,1344]{1,0:T(8,128)S(1)} %get-tuple-element.5, f32[160]{0:T(256)S(1)} %convert_element_type.38), kind=kOutput, calls=%fused_computation.6 | convolution fusion | flops 2645544960 | bytes 20202112 | tf_op jit(solution)/shard_map/dot_general | solution.py:46
  137.7 9.9 %all-reduce.1 = bf16[160]{0:T(256)(128)(2,1)S(1)} all-reduce(f32[160]{0:T(256)S(1)} %get-tuple-element.4), channel_id=3, replica_groups=mesh['expert'=8,'blk'=4] {'blk'}, use_global_device_ids=true, to_apply=%region_3.0.clone | all-reduce | flops 160 | bytes 960
  148.4 3.4 %all-to-all-start.4 = ((bf16[8,5,1]{1,2,0:T(2,128)(2,1)}), bf16[8,5,1]{1,2,0:T(2,128)(2,1)S(1)}, u32[]{:S(2)}, u32[]{:S(2)}) async-start(bf16[8,5,1]{1,2,0:T(2,128)(2,1)} %all_to_all.56), calls=%async_computation.5 | async-start | bytes 8192 | tf_op jit(solution)/shard_map/all_to_all | solution.py:54
  151.8 25.9 %reduce-scatter.2.cloned.1.call-done = bf16[40,6144]{1,0:T(8,128)(2,1)} async-done(((bf16[160,6144]{1,0:T(8,128)(2,1)}), bf16[40,6144]{1,0:T(8,128)(2,1)}) %reduce-scatter.2.cloned.1.call-update) | async-done | bytes 491536 | tf_op jit(solution)/shard_map/reduce_scatter | solution.py:45
  177.7 2.1 %all_to_all.49 = bf16[8,5,6144]{2,1,0:T(8,128)(2,1)} reshape(bf16[40,6144]{1,0:T(8,128)(2,1)} %reduce-scatter.2.cloned.1.call-done) | data formatting | bytes 983040 | tf_op jit(solution)/shard_map/all_to_all | solution.py:53
  179.8 3.7 %all-to-all-start.3 = ((bf16[8,5,6144]{2,1,0:T(8,128)(2,1)}), bf16[8,5,6144]{2,1,0:T(8,128)(2,1)S(1)}, u32[]{:S(2)}, u32[]{:S(2)}) async-start(bf16[8,5,6144]{2,1,0:T(8,128)(2,1)} %all_to_all.49), calls=%async_computation.4 | async-start | bytes 1572864 | tf_op jit(solution)/shard_map/all_to_all | solution.py:53
  184.3 11.7 %all-to-all-done.3 = bf16[8,5,6144]{2,1,0:T(8,128)(2,1)S(1)} async-done(((bf16[8,5,6144]{2,1,0:T(8,128)(2,1)}), bf16[8,5,6144]{2,1,0:T(8,128)(2,1)S(1)}, u32[]{:S(2)}, u32[]{:S(2)}) %all-to-all-start.3) | async-done | bytes 491552 | tf_op jit(solution)/shard_map/all_to_all | solution.py:53
  196.2 0.8 convolution_convert_fusion.2
  (25 shorter events, 3.3 us)
Async XLA Ops:
  7.2 0.9 copy-start
  7.2 63.3 %all-gather.5.cloned.1.call-start = ((), (), s32[]{:S(2)}) async-start(), calls=%async_computation.7 | async-start | bytes 2457600 | tf_op jit(solution)/shard_map/all_gather | solution.py:39
  27.2 87.2 %all-gather.3.cloned.1.call-start = ((), (), s32[]{:S(2)}) async-start(), calls=%async_computation.6 | async-start | bytes 2457600 | tf_op jit(solution)/shard_map/all_gather | solution.py:40
  46.2 7.9 %all-to-all-start = ((bf16[8,5,1]{1,2,0:T(2,128)(2,1)}), bf16[8,5,1]{1,2,0:T(2,128)(2,1)S(1)}, u32[]{:S(2)}, u32[]{:S(2)}) async-start(bf16[8,5,1]{1,2,0:T(2,128)(2,1)} %all_to_all.55), calls=%async_computation | async-start | bytes 8192 | tf_op jit(solution)/shard_map/all_to_all | solution.py:34
  49.5 128.1 %reduce-scatter.2.cloned.1.call-start = ((), (), s32[]{:S(2)}) async-start(), calls=%async_computation.8 | async-start | bytes 2457600 | tf_op jit(solution)/shard_map/reduce_scatter | solution.py:45
  148.4 31.4 %all-to-all-start.4 = ((bf16[8,5,1]{1,2,0:T(2,128)(2,1)}), bf16[8,5,1]{1,2,0:T(2,128)(2,1)S(1)}, u32[]{:S(2)}, u32[]{:S(2)}) async-start(bf16[8,5,1]{1,2,0:T(2,128)(2,1)} %all_to_all.56), calls=%async_computation.5 | async-start | bytes 8192 | tf_op jit(solution)/shard_map/all_to_all | solution.py:54
  179.8 16.2 %all-to-all-start.3 = ((bf16[8,5,6144]{2,1,0:T(8,128)(2,1)}), bf16[8,5,6144]{2,1,0:T(8,128)(2,1)S(1)}, u32[]{:S(2)}, u32[]{:S(2)}) async-start(bf16[8,5,6144]{2,1,0:T(8,128)(2,1)} %all_to_all.49), calls=%async_computation.4 | async-start | bytes 1572864 | tf_op jit(solution)/shard_map/all_to_all | solution.py:53
Sparse Core Ops, SparseCore 0:
  27.3 43.1 all-gather.4
  72.0 42.3 all-gather.2
  137.2 40.4 reduce-scatter.1
where the time goes:
time: 204 us
  waiting for transfers between devices  75.3 us (37%)
  blocking collectives  55.2 us (27%)
  matrix products  38.2 us (19%)
  between operations  15 us (7%)
  starting transfers between devices  10.4 us (5%)
  local copies, waits for them, and re-layouts  8.07 us (4%)
    all_gather x1, waiting for transfers between devices, per_device(): lax.all_gather(recv_dy, 'blk', axis=0, tiled=True)  31.9 us
    reduce_scatter x1, waiting for transfers between devices, per_device(): lax.psum_scatter(jnp.dot(piece_slope, weight_in, preferred_element_type=j...  25.9 us
    unnamed x2, blocking collectives  22.7 us
    all_to_all x1, blocking collectives, per_device(): lax.all_to_all(send_x, 'expert', split_axis=0, concat_axis=0, tiled=True)  17.5 us
    all_to_all x1, blocking collectives, per_device(): lax.all_to_all(send_dy, 'expert', split_axis=0, concat_axis=0, tiled=True)  14.9 us
    dot_general x1, matrix products, hidden_terms(): lax.dot_general(rows_dy, weight_down, contract, preferred_element_type=jn...  12.2 us
    dot_general x1, matrix products, hidden_terms(): lax.dot_general(rows_x, weight_in, contract, preferred_element_type=jnp.f...  12.1 us
    all_to_all x1, waiting for transfers between devices, per_device(): lax.all_to_all(grad_rows, 'expert', split_axis=0, concat_axis=0, tiled=True)  11.7 us
  transfers between devices with their start and end apart: 6, of which 5 were waited for; matrix products, arithmetic and copies ran while one was open for 8% of the time, Pallas kernels for 0%

commit v1 on v0

v1 whole, which is shorter than its diff:
```python
import functools

import jax
import jax.numpy as jnp
from jax import lax
from jax.experimental import pallas as pl
from jax.experimental.pallas import tpu as pltpu
from jax.sharding import PartitionSpec as P


LANES = 128
AXES = ("expert", "blk")
F32 = jnp.float32
BF16 = jnp.bfloat16
VMEM = pl.BlockSpec(memory_space=pltpu.VMEM)
HBM = pl.BlockSpec(memory_space=pltpu.HBM)
CONTRACT_LAST = (((1,), (1,)), ((), ()))


def hidden_terms(rows_x, rows_dy, rows_gate, weight_in, weight_down):
    pre = lax.dot_general(rows_x, weight_in, CONTRACT_LAST, preferred_element_type=F32)
    back = lax.dot_general(rows_dy, weight_down, CONTRACT_LAST, preferred_element_type=F32)
    sigma = jax.nn.sigmoid(pre)
    gate_part = jnp.sum(pre * sigma * back, axis=1)
    slope = rows_gate.astype(F32)[:, None] * back * sigma * (1.0 + pre * (1.0 - sigma))
    return (slope.astype(BF16), gate_part)


def routed_device(tokens, out_grad, expert_ids, slots, gates, w_in, w_down):
    tok_count = tokens.shape[0]
    top_count = expert_ids.shape[1]
    expert_count = lax.axis_size("expert")
    capacity = max(2, (tok_count * top_count + expert_count - 1) // expert_count + 1)
    slot_count = expert_count * capacity
    target = expert_ids * capacity + slots
    matches = (
        target[None, :, :] == jnp.arange(slot_count, dtype=jnp.int32)[:, None, None]
    ).astype(F32)
    placing = jnp.sum(matches, axis=2).astype(BF16)
    send_x = jnp.dot(placing, tokens, preferred_element_type=F32).astype(BF16)
    send_dy = jnp.dot(placing, out_grad, preferred_element_type=F32).astype(BF16)
    send_gate = jnp.einsum("stk,tk->s", matches, gates.astype(F32)).astype(BF16)
    recv_x, recv_dy, recv_gate = (
        lax.all_to_all(send_x, "expert", split_axis=0, concat_axis=0, tiled=True),
        lax.all_to_all(send_dy, "expert", split_axis=0, concat_axis=0, tiled=True),
        lax.all_to_all(send_gate, "expert", split_axis=0, concat_axis=0, tiled=True),
    )
    weight_in = w_in[0]
    weight_down = w_down[0]
    piece_slope, piece_gate = hidden_terms(
        lax.all_gather(recv_x, "blk", axis=0, tiled=True),
        lax.all_gather(recv_dy, "blk", axis=0, tiled=True),
        lax.all_gather(recv_gate, "blk", axis=0, tiled=True),
        weight_in,
        weight_down,
    )
    grad_rows = lax.psum_scatter(
        jnp.dot(piece_slope, weight_in, preferred_element_type=F32).astype(BF16),
        "blk",
        scatter_dimension=0,
        tiled=True,
    )
    gate_rows = lax.psum_scatter(piece_gate, "blk", scatter_dimension=0, tiled=True)
    back_rows, back_gate = (
        lax.all_to_all(grad_rows, "expert", split_axis=0, concat_axis=0, tiled=True),
        lax.all_to_all(
            gate_rows.astype(BF16), "expert", split_axis=0, concat_axis=0, tiled=True
        ),
    )
    grad_tokens = lax.dot_general(
        placing, back_rows, (((0,), (0,)), ((), ())), preferred_element_type=F32
    ).astype(BF16)
    grad_gates = jnp.einsum("stk,s->tk", matches, back_gate.astype(F32)).astype(BF16)
    return (grad_tokens, grad_gates)


class Ring:
    def __init__(self, experts, blocks):
        self.experts, self.blocks = experts, blocks
        self.plane = experts // 2

    def move(self, array, step):
        pairs = []
        for e in range(self.experts):
            for z in range(self.blocks):
                to_e, to_z = step(e, z)
                pairs.append((e * self.blocks + z, to_e * self.blocks + to_z))
        return lax.ppermute(array, AXES, pairs)

    def core(self, array):
        return self.move(array, lambda e, z: (e ^ 1, z))

    def to(self, array, stage, k):
        if stage == "plane":
            return self.move(array, lambda e, z: (e ^ (2 * k), z))
        return self.move(array, lambda e, z: (e, z ^ k))

    def count(self, stage):
        return self.plane if stage == "plane" else self.blocks

    def gather(self, array, stage):
        others = [self.to(array, stage, k) for k in range(1, self.count(stage))]
        return jnp.concatenate([array] + others, axis=0)

    def scatter(self, parts, stage):
        return [parts[0]] + [self.to(parts[k], stage, k) for k in range(1, self.count(stage))]


def add_up(parts):
    total = parts[0].astype(F32)
    for part in parts[1:]:
        total = total + part.astype(F32)
    return total


def params(mib):
    return pltpu.CompilerParams(vmem_limit_bytes=mib << 20)


def cost(rows, hidden, width):
    return pl.CostEstimate(
        flops=2 * rows * hidden * width, bytes_accessed=hidden * width * 2, transcendentals=0
    )


def column_blocks(hidden):
    return [(at, min(at + 256, hidden)) for at in range(0, hidden, 256)]


def times(rows, weight):
    return lax.dot_general(rows, weight, CONTRACT_LAST, preferred_element_type=F32)


def prepare_kernel(cut, *refs):
    tokens, out_grad, ids, gates, wide_x, wide_dy, narrow, rows_x, rows_dy, sems = refs
    copies = [
        pltpu.make_async_copy(tokens, rows_x, sems.at[0]),
        pltpu.make_async_copy(out_grad, rows_dy, sems.at[1]),
    ]
    for copy in copies:
        copy.start()
    tok, width = rows_x.shape
    expert = lax.broadcasted_iota(jnp.int32, (LANES, tok), 0)
    table = jnp.zeros((LANES, tok), F32)
    for k in range(ids.shape[0]):
        gate = gates[k : k + 1, :].astype(F32)
        table = table + jnp.where(expert == ids[k : k + 1, :], gate, 0.0)
    narrow[:tok, width - cut :] = jnp.zeros((tok, LANES), BF16)
    narrow[tok:, width - cut :] = table.T.astype(BF16)
    copies[0].wait()
    wide_x[...] = rows_x[:, :cut]
    narrow[:tok, : width - cut] = rows_x[:, cut:]
    copies[1].wait()
    wide_dy[...] = rows_dy[:, :cut]
    narrow[tok:, : width - cut] = rows_dy[:, cut:]


def prepare(tokens, out_grad, ids, gates, cut):
    tok, width = tokens.shape
    wide = jax.ShapeDtypeStruct((tok, cut), BF16)
    return pl.pallas_call(
        functools.partial(prepare_kernel, cut),
        out_shape=(wide, wide, jax.ShapeDtypeStruct((2 * tok, width - cut + LANES), BF16)),
        in_specs=[HBM, HBM, VMEM, VMEM],
        out_specs=(VMEM,) * 3,
        scratch_shapes=[pltpu.VMEM((tok, width), BF16)] * 2
        + [pltpu.SemaphoreType.DMA((2,))],
        compiler_params=params(2),
    )(in_hbm(tokens), in_hbm(out_grad), ids.T, gates.T)


def in_hbm(array):
    return pltpu.with_memory_space_constraint(array, pltpu.HBM)


def stack(own, other, rows):
    half = own.shape[0]
    rows[:half, :] = own[...]
    rows[half:, :] = other[...]


def load_kernel(source, _, held, sem):
    copy = pltpu.make_async_copy(source, held, sem)
    copy.start()
    copy.wait()


def load(weight, after, grant):
    return pl.pallas_call(
        load_kernel,
        out_shape=jax.ShapeDtypeStruct(weight.shape, BF16),
        in_specs=[HBM, pl.BlockSpec(memory_space=pl.ANY)],
        out_specs=VMEM,
        scratch_shapes=[pltpu.SemaphoreType.DMA],
        compiler_params=params(grant),
        cost_estimate=cost(0, *weight.shape),
    )(weight, after)


def first_kernel(own, other, weight, pre, rows):
    width = own.shape[1]
    stack(own, other, rows)
    for at, to in column_blocks(weight.shape[0]):
        pre[:, at:to] = times(rows[...], weight[at:to, :width])


def first_product(own, other, weight):
    half, width = own.shape
    hidden = weight.shape[0]
    return pl.pallas_call(
        first_kernel,
        out_shape=jax.ShapeDtypeStruct((2 * half, hidden), F32),
        in_specs=[VMEM, VMEM, VMEM],
        out_specs=VMEM,
        scratch_shapes=[pltpu.VMEM((2 * half, width), BF16)],
        compiler_params=params(LAST_GRANT),
        cost_estimate=cost(2 * half, hidden, width),
    )(own, other, weight)


def last_kernel(plane, blocks, tok, *refs):
    pre_ref, n_own, n_other, own, other, weight_in, weight_down = refs[:7]
    slope_ref, part_ref, rows, rows_x, rows_dy, table = refs[7:]
    cut, rest = rows.shape[1], rows_x.shape[1]
    stack(own, other, rows)
    for c, ref in enumerate((n_own, n_other)):
        for z in range(blocks):
            for p in range(plane):
                at = (z * plane + p) * 2 * tok
                to = ((c * plane + p) * blocks + z) * tok
                rows_x[to : to + tok, :] = ref[at : at + tok, :rest]
                rows_dy[to : to + tok, :] = ref[at + tok : at + 2 * tok, :rest]
                table[to : to + tok, :] = ref[at + tok : at + 2 * tok, rest:].astype(F32)
    lane = lax.broadcasted_iota(jnp.int32, (1, LANES), 1)
    mask = (lane == lax.axis_index("expert")).astype(F32)
    gate = jnp.sum(table[...] * mask, axis=1, keepdims=True)
    total = jnp.zeros((rows.shape[0], 1), F32)
    for at, to in column_blocks(weight_in.shape[0]):
        pre = pre_ref[:, at:to] + times(rows_x[...], weight_in[at:to, cut:])
        back = times(rows_dy[...], weight_down[at:to, cut:])
        back = back + times(rows[...], weight_down[at:to, :cut])
        sigma = jax.nn.sigmoid(pre)
        total = total + jnp.sum(pre * sigma * back, axis=1, keepdims=True)
        slope = gate * back * sigma * (1.0 + pre * (1.0 - sigma))
        slope_ref[:, at:to] = slope.astype(BF16)
    part_ref[...] = (total * mask).astype(BF16)


def last_product(pre, n_own, n_other, own, other, weight_in, weight_down, ring, tok):
    rows, hidden = pre.shape
    width = weight_in.shape[1]
    cut = own.shape[1]
    return pl.pallas_call(
        functools.partial(last_kernel, ring.plane, ring.blocks, tok),
        out_shape=(
            jax.ShapeDtypeStruct((rows, hidden), BF16),
            jax.ShapeDtypeStruct((rows, LANES), BF16),
        ),
        in_specs=[VMEM] * 7,
        out_specs=(VMEM, VMEM),
        scratch_shapes=[
            pltpu.VMEM((rows, cut), BF16),
            pltpu.VMEM((rows, width - cut), BF16),
            pltpu.VMEM((rows, width - cut), BF16),
            pltpu.VMEM((rows, LANES), F32),
        ],
        compiler_params=params(LAST_GRANT),
        cost_estimate=cost(rows, hidden, 2 * width - cut),
    )(pre, n_own, n_other, own, other, weight_in, weight_down)


def spread_kernel(lo, hi, *refs):
    slope, weight, *extra, own, other = refs
    half = own.shape[0]
    value = slope[...]
    for at in range(lo, hi, 512):
        to = min(at + 512, hi)
        out = jnp.dot(value, weight[:, at:to], preferred_element_type=F32).astype(BF16)
        own[:, at - lo : to - lo] = out[:half]
        other[:, at - lo : to - lo] = out[half:]
    for ref in extra:
        own[:, hi - lo :] = ref[:half, :]
        other[:, hi - lo :] = ref[half:, :]


def spread(slope, weight, lo, hi, extra):
    rows, hidden = slope.shape
    half = jax.ShapeDtypeStruct((rows // 2, hi - lo + LANES * len(extra)), BF16)
    return pl.pallas_call(
        functools.partial(spread_kernel, lo, hi),
        out_shape=(half, half),
        in_specs=[VMEM, VMEM] + [VMEM] * len(extra),
        out_specs=(VMEM, VMEM),
        compiler_params=params(GRANT),
        cost_estimate=cost(rows, hidden, hi - lo),
    )(slope, weight, *extra)


def core_sums(ring, own, other, stage, tok):
    width = own.shape[1]
    shape = (ring.plane, ring.blocks, tok, width)
    parts = [own.reshape(shape), ring.core(other).reshape(shape)]
    axis = 0 if stage == "plane" else 1
    return [
        add_up([lax.slice_in_dim(part, k, k + 1, axis=axis) for part in parts])
        .astype(BF16)
        .reshape(-1, width)
        for k in range(ring.count(stage))
    ]


def regroup(parts, count):
    rows = parts[0].shape[0] // count
    return [add_up([p[k * rows : (k + 1) * rows] for p in parts]) for k in range(count)]


def dense_device(tokens, out_grad, expert_ids, slots, gates, w_in, w_down):
    tok, width = tokens.shape
    ring = Ring(lax.axis_size("expert"), lax.axis_size("blk"))
    cut = cut_of(width)
    lanes = jnp.arange(LANES, dtype=jnp.int32)
    weight_in, weight_down = in_hbm(w_in[0]), in_hbm(w_down[0])
    wide_x, wide_dy, narrow = prepare(tokens, out_grad, expert_ids, gates, cut)
    x_line = ring.gather(wide_x, "line")
    n_plane = ring.gather(narrow, "plane")
    x_own = ring.gather(x_line, "plane")
    dy_line = ring.gather(wide_dy, "line")
    n_own = ring.gather(n_plane, "line")
    dy_own = ring.gather(dy_line, "plane")
    held_in = load(weight_in, x_line, LOAD_GRANT)
    x_other = ring.core(x_own)
    pre = first_product(x_own, x_other, held_in)
    held_down = load(weight_down, pre, DOWN_GRANT)
    n_other = ring.core(n_own)
    dy_other = ring.core(dy_own)
    slope, part = last_product(pre, n_own, n_other, dy_own, dy_other, held_in, held_down, ring, tok)

    chosen = (expert_ids[:, :, None] == lanes[None, None, :]).astype(F32)
    chosen = lax.optimization_barrier(chosen)
    mid = cut // 2 // 256 * 256
    own1, other1 = spread(slope, held_in, 0, mid, ())
    own2, other2 = spread(slope, held_in, mid, cut, ())
    own3, other3 = spread(slope, held_in, cut, width, (part,))
    plane1 = ring.scatter(core_sums(ring, own1, other1, "plane", tok), "plane")
    plane2 = ring.scatter(core_sums(ring, own2, other2, "plane", tok), "plane")
    line3 = ring.scatter(core_sums(ring, own3, other3, "line", tok), "line")
    wide = [
        jnp.concatenate(both, axis=1).astype(BF16)
        for both in zip(regroup(plane1, ring.blocks), regroup(plane2, ring.blocks))
    ]
    rest = [block.astype(BF16) for block in regroup(line3, ring.plane)]
    sum_wide = add_up(ring.scatter(wide, "line"))
    sum_rest = add_up(ring.scatter(rest, "plane"))
    grad_tokens = jnp.concatenate([sum_wide, sum_rest[:, : width - cut]], axis=1)
    grad_gates = jnp.sum(chosen * sum_rest[:, None, width - cut :], axis=2)
    return grad_tokens.astype(BF16), grad_gates.astype(BF16)


def cut_of(width):
    return width * 19 // 24 // 256 * 256


GRANT = 8
LOAD_GRANT = 4
DOWN_GRANT = 4
LAST_GRANT = 8


def power_of_two(n):
    return n & (n - 1) == 0


def fits(tokens, w_in, mesh):
    experts, blocks = mesh.shape["expert"], mesh.shape["blk"]
    count, width = tokens.shape
    held = 2 * (w_in.shape[1] // blocks) * width * 2 + 4 * count * width * 2
    return (
        power_of_two(experts)
        and power_of_two(blocks)
        and 2 < experts <= LANES
        and blocks > 1
        and width % 1024 == 0
        and count == 8 * experts * blocks
        and held <= 48 << 20
    )


def solution(mesh):
    def program(tokens, out_grad, expert_ids, slots, gates, w_in, w_down):
        dense = fits(tokens, w_in, mesh)
        rows = P(AXES, None)
        weights = P("expert", "blk", None)
        step = jax.shard_map(
            dense_device if dense else routed_device,
            mesh=mesh,
            in_specs=(rows, rows, rows, rows, rows, weights, weights),
            out_specs=(rows, rows),
            check_vma=False,
        )
        return step(tokens, out_grad, expert_ids, slots, gates, w_in, w_down)

    return program
```

time: 204 us -> 147 us (0.72)
  blocking collectives: 55.2 us -> 0 us
  starting transfers between devices: 10.4 us -> 54.4 us
  matrix products: 38.2 us -> 0 us
  Pallas kernels: 0 us -> 28.2 us
  waiting for transfers between devices: 75.3 us -> 59.5 us
  between operations: 15 us -> 1.07 us
  local copies, waits for them, and re-layouts: 8.07 us -> 1.71 us
    ppermute x0 -> x39, waiting for transfers between devices: none -> 59.5 us  [move(): return lax.ppermute(array, AXES, pairs)]
    ppermute x0 -> x39, starting transfers between devices: none -> 54.4 us  [move(): return lax.ppermute(array, AXES, pairs)]
    dot_general x8 -> x0, matrix products: 38.2 us -> none  [the longest x1 12.2 us: hidden_terms(): lax.dot_general(rows_dy, weight_down, contract, preferred_element_type=jn...]
    all_gather x2 -> x0, waiting for transfers between devices: 35.1 us -> none  [the longest x1 31.9 us: per_device(): lax.all_gather(recv_dy, 'blk', axis=0, tiled=True)]
    all_to_all x2 -> x0, blocking collectives: 32.5 us -> none  [the longest x1 17.5 us: per_device(): lax.all_to_all(send_x, 'expert', split_axis=0, concat_axis=0, tiled=True)]
    pallas_call x0 -> x8, Pallas kernels: none -> 28.2 us  [the longest x2 11.4 us: load(): pl.pallas_call(load_kernel, out_shape=jax.ShapeDtypeStruct(weight.shape,...]
    reduce_scatter x1 -> x0, waiting for transfers between devices: 25.9 us -> none  [per_device(): lax.psum_scatter(jnp.dot(piece_slope, weight_in, preferred_element_type=j...]
    unnamed x2 -> x0, blocking collectives: 22.7 us -> none
  transfers between devices with their start and end apart: 6 -> 39, of which waited for: 5 -> 19; matrix products, arithmetic and copies ran while one was open for 8% -> 1% of each run, Pallas kernels for 0% -> 13%
where the time goes in v1:
time: 147 us
  waiting for transfers between devices  59.5 us (40%)
  starting transfers between devices  54.4 us (37%)
  Pallas kernels  28.2 us (19%)
  other arithmetic  2.04 us (1%)
  local copies, waits for them, and re-layouts  1.71 us (1%)
    ppermute x39, waiting for transfers between devices, move(): return lax.ppermute(array, AXES, pairs)  59.5 us
    ppermute x39, starting transfers between devices, move(): return lax.ppermute(array, AXES, pairs)  54.4 us
    pallas_call x2, Pallas kernels, load(): pl.pallas_call(load_kernel, out_shape=jax.ShapeDtypeStruct(weight.shape,...  11.4 us
    pallas_call x1, Pallas kernels, last_product(): pl.pallas_call(functools.partial(last_kernel, ring.plane, ring.blocks, to...  6.44 us
    pallas_call x3, Pallas kernels, spread(): pl.pallas_call(functools.partial(spread_kernel, lo, hi), out_shape=(half,...  5.39 us
    pallas_call x1, Pallas kernels, first_product(): pl.pallas_call(first_kernel, out_shape=jax.ShapeDtypeStruct((2 * half, hi...  4.05 us
  transfers between devices with their start and end apart: 39, of which 19 were waited for; matrix products, arithmetic and copies ran while one was open for 1% of the time, Pallas kernels for 13%

profile of v1, /device:TPU:0, one launch (start us, length us, event | category | flops | bytes accessed | tf_op | source)
XLA Modules:
  0.0 146.9 jit_solution(15869612335565241881)
XLA Ops:
  3.0 3.1 %collective-permute-start.14 = (bf16[8,4864]{1,0:T(8,128)(2,1)S(1)}, bf16[8,4864]{1,0:T(8,128)(2,1)S(1)}, u32[]{:S(2)}, u32[]{:S(2)}) collective-permute-start(bf16[8,4864]{1,0:T(8,128)(2,1)S(1)} %get-tuple-element.15), channel_id=1, source_target_pairs={{0,1},{1,0},{2,3},{3,2},{4,5},{5,4},{6,7},{7,6},{8,9},{9,8},{10,11... | collective-permute-start | bytes 233480 | tf_op jit(solution)/shard_map/ppermute | solution.py:88
  6.1 2.6 %collective-permute-start.15 = (bf16[8,4864]{1,0:T(8,128)(2,1)S(1)}, bf16[8,4864]{1,0:T(8,128)(2,1)S(1)}, u32[]{:S(2)}, u32[]{:S(2)}) collective-permute-start(bf16[8,4864]{1,0:T(8,128)(2,1)S(1)} %get-tuple-element.15), channel_id=1, source_target_pairs={{0,2},{1,3},{2,0},{3,1},{4,6},{5,7},{6,4},{7,5},{8,10},{9,11},{10,... | collective-permute-start | bytes 233480 | tf_op jit(solution)/shard_map/ppermute | solution.py:88
  11.1 2.5 %collective-permute-done.7 = bf16[16,1408]{1,0:T(8,128)(2,1)S(1)} collective-permute-done((bf16[16,1408]{1,0:T(8,128)(2,1)S(1)}, bf16[16,1408]{1,0:T(8,128)(2,1)S(1)}, u32[]{:S(2)}, u32[]{:S(2)}) %collective-permute-start.7) | collective-permute-done | bytes 45088 | tf_op jit(solution)/shard_map/ppermute | solution.py:88
  15.2 2.5 %collective-permute-done.8 = bf16[16,1408]{1,0:T(8,128)(2,1)S(1)} collective-permute-done((bf16[16,1408]{1,0:T(8,128)(2,1)S(1)}, bf16[16,1408]{1,0:T(8,128)(2,1)S(1)}, u32[]{:S(2)}, u32[]{:S(2)}) %collective-permute-start.8) | collective-permute-done | bytes 45088 | tf_op jit(solution)/shard_map/ppermute | solution.py:88
  17.7 2.4 %collective-permute-start.9 = (bf16[16,1408]{1,0:T(8,128)(2,1)S(1)}, bf16[16,1408]{1,0:T(8,128)(2,1)S(1)}, u32[]{:S(2)}, u32[]{:S(2)}) collective-permute-start(bf16[16,1408]{1,0:T(8,128)(2,1)S(1)} %get-tuple-element.14), channel_id=1, source_target_pairs={{0,24},{1,25},{2,26},{3,27},{4,28},{5,29},{6,30},{7,31},{8,16},{9,... | collective-permute-start | bytes 135176 | tf_op jit(solution)/shard_map/ppermute | solution.py:88
  20.1 2.5 %collective-permute-done.9 = bf16[16,1408]{1,0:T(8,128)(2,1)S(1)} collective-permute-done((bf16[16,1408]{1,0:T(8,128)(2,1)S(1)}, bf16[16,1408]{1,0:T(8,128)(2,1)S(1)}, u32[]{:S(2)}, u32[]{:S(2)}) %collective-permute-start.9) | collective-permute-done | bytes 45088 | tf_op jit(solution)/shard_map/ppermute | solution.py:88
  22.6 3.5 %collective-permute-start.1 = (bf16[8,4864]{1,0:T(8,128)(2,1)S(1)}, bf16[8,4864]{1,0:T(8,128)(2,1)S(1)}, u32[]{:S(2)}, u32[]{:S(2)}) collective-permute-start(bf16[8,4864]{1,0:T(8,128)(2,1)S(1)} %get-tuple-element.13), channel_id=1, source_target_pairs={{0,2},{1,3},{2,0},{3,1},{4,6},{5,7},{6,4},{7,5},{8,10},{9,11},{10,... | collective-permute-start | bytes 233480 | tf_op jit(solution)/shard_map/ppermute | solution.py:88
  26.9 3.9 %collective-permute-start.11 = (bf16[64,1408]{1,0:T(8,128)(2,1)S(1)}, bf16[64,1408]{1,0:T(8,128)(2,1)S(1)}, u32[]{:S(2)}, u32[]{:S(2)}) collective-permute-start(bf16[64,1408]{1,0:T(8,128)(2,1)S(1)} %get-tuple-element.63), channel_id=1, source_target_pairs={{0,2},{1,3},{2,0},{3,1},{4,6},{5,7},{6,4},{7,5},{8,10},{9,11},{10,... | collective-permute-start | bytes 540680 | tf_op jit(solution)/shard_map/ppermute | solution.py:88
  30.9 3.9 %collective-permute-done.1 = bf16[8,4864]{1,0:T(8,128)(2,1)S(1)} collective-permute-done((bf16[8,4864]{1,0:T(8,128)(2,1)S(1)}, bf16[8,4864]{1,0:T(8,128)(2,1)S(1)}, u32[]{:S(2)}, u32[]{:S(2)}) %collective-permute-start.1) | collective-permute-done | bytes 77856 | tf_op jit(solution)/shard_map/ppermute | solution.py:88
  37.9 3.8 %collective-permute-done.17 = bf16[32,4864]{1,0:T(8,128)(2,1)S(1)} collective-permute-done((bf16[32,4864]{1,0:T(8,128)(2,1)S(1)}, bf16[32,4864]{1,0:T(8,128)(2,1)S(1)}, u32[]{:S(2)}, u32[]{:S(2)}) %collective-permute-start.17) | collective-permute-done | bytes 311328 | tf_op jit(solution)/shard_map/ppermute | solution.py:88
  43.2 5.4 %collective-permute-done.3 = bf16[32,4864]{1,0:T(8,128)(2,1)S(1)} collective-permute-done((bf16[32,4864]{1,0:T(8,128)(2,1)S(1)}, bf16[32,4864]{1,0:T(8,128)(2,1)S(1)}, u32[]{:S(2)}, u32[]{:S(2)}) %collective-permute-start.3) | collective-permute-done | bytes 311328 | tf_op jit(solution)/shard_map/ppermute | solution.py:88
  50.1 6.8 %collective-permute-done.4 = bf16[32,4864]{1,0:T(8,128)(2,1)S(1)} collective-permute-done((bf16[32,4864]{1,0:T(8,128)(2,1)S(1)}, bf16[32,4864]{1,0:T(8,128)(2,1)S(1)}, u32[]{:S(2)}, u32[]{:S(2)}) %collective-permute-start.4) | collective-permute-done | bytes 311328 | tf_op jit(solution)/shard_map/ppermute | solution.py:88
  58.4 6.3 %collective-permute-done.5 = bf16[32,4864]{1,0:T(8,128)(2,1)S(1)} collective-permute-done((bf16[32,4864]{1,0:T(8,128)(2,1)S(1)}, bf16[32,4864]{1,0:T(8,128)(2,1)S(1)}, u32[]{:S(2)}, u32[]{:S(2)}) %collective-permute-start.5) | collective-permute-done | bytes 311328 | tf_op jit(solution)/shard_map/ppermute | solution.py:88
  66.3 6.2 %collective-permute-done.19 = bf16[32,4864]{1,0:T(8,128)(2,1)S(1)} collective-permute-done((bf16[32,4864]{1,0:T(8,128)(2,1)S(1)}, bf16[32,4864]{1,0:T(8,128)(2,1)S(1)}, u32[]{:S(2)}, u32[]{:S(2)}) %collective-permute-start.19) | collective-permute-done | bytes 311328 | tf_op jit(solution)/shard_map/ppermute | solution.py:88
  73.2 5.7 %shard_map.78.weight.refs_5_.refs_1_ = bf16[1344,6144]{1,0:T(8,128)(2,1)S(1)} custom-call(bf16[1344,6144]{1,0:T(8,128)(2,1)} %bitcast.79, bf16[32,4864]{1,0:T(8,128)(2,1)S(1)} %get-tuple-element.55._), custom_call_target="tpu_custom_call" | custom-call | bytes 16515072 | tf_op jit(solution)/shard_map/pallas_call | solution.py:189
  78.9 4.1 %shard_map.79._.refs_0_ = f32[256,1344]{1,0:T(8,128)S(1)} custom-call(bf16[128,4864]{1,0:T(8,128)(2,1)S(1)} %constant_dynamic-update-slice_fusion.4.own, bf16[128,4864]{1,0:T(8,128)(2,1)S(1)} %collective-permute-done.6.other, bf16[1344,6144]{1,0:T(8,128)(2,1)S(1)} %shard_map.78.weight.refs_5_.refs_1_), custom_call_target="tpu_custom_call" | custom-call | flops 3347054592 | bytes 13074432 | tf_op jit(solution)/shard_map/pallas_call | solution.py:210
  83.0 5.7 %shard_map.80.refs_6_ = bf16[1344,6144]{1,0:T(8,128)(2,1)S(1)} custom-call(bf16[1344,6144]{1,0:T(8,128)(2,1)} %bitcast.80, f32[256,1344]{1,0:T(8,128)S(1)} %shard_map.79._.refs_0_), custom_call_target="tpu_custom_call" | custom-call | bytes 16515072 | tf_op jit(solution)/shard_map/pallas_call | solution.py:189
  88.7 6.4 %shard_map.81 = (bf16[256,1344]{1,0:T(8,128)(2,1)S(1)}, bf16[256,128]{1,0:T(8,128)(2,1)S(1)}) custom-call(f32[256,1344]{1,0:T(8,128)S(1)} %shard_map.79._.refs_0_, bf16[256,1408]{1,0:T(8,128)(2,1)S(1)} %constant_dynamic-update-slice_fusion.15.refs_1_, bf16[256,1408]{1,0:T(8,128)(2,1)S(1)} %collective-permute-done.13.refs_2_, ...), custom_call_target="tpu_custom_call" | custom-call | flops 5108662272 | bytes 19955712 | tf_op jit(solution)/shard_map/pallas_call | solution.py:253
  98.2 5.4 %collective-permute-start.33 = (bf16[32,1408]{1,0:T(8,128)(2,1)S(1)}, bf16[32,1408]{1,0:T(8,128)(2,1)S(1)}, u32[]{:S(2)}, u32[]{:S(2)}) collective-permute-start(bf16[32,1408]{1,0:T(8,128)(2,1)S(1)} %get-tuple-element.35), channel_id=1, source_target_pairs={{0,1},{1,0},{2,3},{3,2},{4,5},{5,4},{6,7},{7,6},{8,9},{9,8},{10,11... | collective-permute-start | bytes 270344 | tf_op jit(solution)/shard_map/ppermute | solution.py:88
  103.6 2.6 %collective-permute-start.35 = (bf16[32,1408]{1,0:T(8,128)(2,1)S(1)}, bf16[32,1408]{1,0:T(8,128)(2,1)S(1)}, u32[]{:S(2)}, u32[]{:S(2)}) collective-permute-start(bf16[32,1408]{1,0:T(8,128)(2,1)S(1)} %get-tuple-element.33), channel_id=1, source_target_pairs={{0,3},{1,2},{2,1},{3,0},{4,7},{5,6},{6,5},{7,4},{8,11},{9,10},{10,... | collective-permute-start | bytes 270344 | tf_op jit(solution)/shard_map/ppermute | solution.py:88
  108.4 4.5 %collective-permute-done.34 = bf16[32,1408]{1,0:T(8,128)(2,1)S(1)} collective-permute-done((bf16[32,1408]{1,0:T(8,128)(2,1)S(1)}, bf16[32,1408]{1,0:T(8,128)(2,1)S(1)}, u32[]{:S(2)}, u32[]{:S(2)}) %collective-permute-start.34) | collective-permute-done | bytes 90144 | tf_op jit(solution)/shard_map/ppermute | solution.py:88
  132.7 3.9 %collective-permute-done.27 = bf16[32,2560]{1,0:T(8,128)(2,1)S(1)} collective-permute-done((bf16[32,2560]{1,0:T(8,128)(2,1)S(1)}, bf16[32,2560]{1,0:T(8,128)(2,1)S(1)}, u32[]{:S(2)}, u32[]{:S(2)}) %collective-permute-start.27) | collective-permute-done | bytes 163872 | tf_op jit(solution)/shard_map/ppermute | solution.py:88
  136.8 2.5 %collective-permute-start.29 = (bf16[8,4864]{1,0:T(8,128)(2,1)S(1)}, bf16[8,4864]{1,0:T(8,128)(2,1)S(1)}, u32[]{:S(2)}, u32[]{:S(2)}) collective-permute-start(bf16[8,4864]{1,0:T(8,128)(2,1)S(1)} %pad_maximum_fusion.1), channel_id=1, source_target_pairs={{0,1},{1,0},{2,3},{3,2},{4,5},{5,4},{6,7},{7,6},{8,9},{9,8},{10,11... | collective-permute-start | bytes 233480 | tf_op jit(solution)/shard_map/ppermute | solution.py:88
  143.3 3.0 %collective-permute-done.30 = bf16[8,4864]{1,0:T(8,128)(2,1)S(1)} collective-permute-done((bf16[8,4864]{1,0:T(8,128)(2,1)S(1)}, bf16[8,4864]{1,0:T(8,128)(2,1)S(1)}, u32[]{:S(2)}, u32[]{:S(2)}) %collective-permute-start.30) | collective-permute-done | bytes 77856 | tf_op jit(solution)/shard_map/ppermute | solution.py:88
  (107 shorter events, 46.8 us)
Async XLA Ops:
  3.0 23.2 %collective-permute-start.14 = (bf16[8,4864]{1,0:T(8,128)(2,1)S(1)}, bf16[8,4864]{1,0:T(8,128)(2,1)S(1)}, u32[]{:S(2)}, u32[]{:S(2)}) collective-permute-start(bf16[8,4864]{1,0:T(8,128)(2,1)S(1)} %get-tuple-element.15), channel_id=1, source_target_pairs={{0,1},{1,0},{2,3},{3,2},{4,5},{5,4},{6,7},{7,6},{8,9},{9,8},{10,11... | collective-permute-start | bytes 233480 | tf_op jit(solution)/shard_map/ppermute | solution.py:88
  6.1 20.1 %collective-permute-start.15 = (bf16[8,4864]{1,0:T(8,128)(2,1)S(1)}, bf16[8,4864]{1,0:T(8,128)(2,1)S(1)}, u32[]{:S(2)}, u32[]{:S(2)}) collective-permute-start(bf16[8,4864]{1,0:T(8,128)(2,1)S(1)} %get-tuple-element.15), channel_id=1, source_target_pairs={{0,2},{1,3},{2,0},{3,1},{4,6},{5,7},{6,4},{7,5},{8,10},{9,11},{10,... | collective-permute-start | bytes 233480 | tf_op jit(solution)/shard_map/ppermute | solution.py:88
  8.7 18.2 %collective-permute-start.16 = (bf16[8,4864]{1,0:T(8,128)(2,1)S(1)}, bf16[8,4864]{1,0:T(8,128)(2,1)S(1)}, u32[]{:S(2)}, u32[]{:S(2)}) collective-permute-start(bf16[8,4864]{1,0:T(8,128)(2,1)S(1)} %get-tuple-element.15), channel_id=1, source_target_pairs={{0,3},{1,2},{2,1},{3,0},{4,7},{5,6},{6,5},{7,4},{8,11},{9,10},{10,... | collective-permute-start | bytes 233480 | tf_op jit(solution)/shard_map/ppermute | solution.py:88
  8.7 22.1 %collective-permute-start = (bf16[8,4864]{1,0:T(8,128)(2,1)S(1)}, bf16[8,4864]{1,0:T(8,128)(2,1)S(1)}, u32[]{:S(2)}, u32[]{:S(2)}) collective-permute-start(bf16[8,4864]{1,0:T(8,128)(2,1)S(1)} %get-tuple-element.13), channel_id=1, source_target_pairs={{0,1},{1,0},{2,3},{3,2},{4,5},{5,4},{6,7},{7,6},{8,9},{9,8},{10,11... | collective-permute-start | bytes 233480 | tf_op jit(solution)/shard_map/ppermute | solution.py:88
  22.6 12.1 %collective-permute-start.1 = (bf16[8,4864]{1,0:T(8,128)(2,1)S(1)}, bf16[8,4864]{1,0:T(8,128)(2,1)S(1)}, u32[]{:S(2)}, u32[]{:S(2)}) collective-permute-start(bf16[8,4864]{1,0:T(8,128)(2,1)S(1)} %get-tuple-element.13), channel_id=1, source_target_pairs={{0,2},{1,3},{2,0},{3,1},{4,6},{5,7},{6,4},{7,5},{8,10},{9,11},{10,... | collective-permute-start | bytes 233480 | tf_op jit(solution)/shard_map/ppermute | solution.py:88
  26.1 10.1 %collective-permute-start.2 = (bf16[8,4864]{1,0:T(8,128)(2,1)S(1)}, bf16[8,4864]{1,0:T(8,128)(2,1)S(1)}, u32[]{:S(2)}, u32[]{:S(2)}) collective-permute-start(bf16[8,4864]{1,0:T(8,128)(2,1)S(1)} %get-tuple-element.13), channel_id=1, source_target_pairs={{0,3},{1,2},{2,1},{3,0},{4,7},{5,6},{6,5},{7,4},{8,11},{9,10},{10,... | collective-permute-start | bytes 233480 | tf_op jit(solution)/shard_map/ppermute | solution.py:88
  26.2 46.3 %collective-permute-start.10 = (bf16[64,1408]{1,0:T(8,128)(2,1)S(1)}, bf16[64,1408]{1,0:T(8,128)(2,1)S(1)}, u32[]{:S(2)}, u32[]{:S(2)}) collective-permute-start(bf16[64,1408]{1,0:T(8,128)(2,1)S(1)} %get-tuple-element.63), channel_id=1, source_target_pairs={{0,1},{1,0},{2,3},{3,2},{4,5},{5,4},{6,7},{7,6},{8,9},{9,8},{10,11... | collective-permute-start | bytes 540680 | tf_op jit(solution)/shard_map/ppermute | solution.py:88
  26.9 45.7 %collective-permute-start.11 = (bf16[64,1408]{1,0:T(8,128)(2,1)S(1)}, bf16[64,1408]{1,0:T(8,128)(2,1)S(1)}, u32[]{:S(2)}, u32[]{:S(2)}) collective-permute-start(bf16[64,1408]{1,0:T(8,128)(2,1)S(1)} %get-tuple-element.63), channel_id=1, source_target_pairs={{0,2},{1,3},{2,0},{3,1},{4,6},{5,7},{6,4},{7,5},{8,10},{9,11},{10,... | collective-permute-start | bytes 540680 | tf_op jit(solution)/shard_map/ppermute | solution.py:88
  30.8 41.8 %collective-permute-start.12 = (bf16[64,1408]{1,0:T(8,128)(2,1)S(1)}, bf16[64,1408]{1,0:T(8,128)(2,1)S(1)}, u32[]{:S(2)}, u32[]{:S(2)}) collective-permute-start(bf16[64,1408]{1,0:T(8,128)(2,1)S(1)} %get-tuple-element.63), channel_id=1, source_target_pairs={{0,3},{1,2},{2,1},{3,0},{4,7},{5,6},{6,5},{7,4},{8,11},{9,10},{10,... | collective-permute-start | bytes 540680 | tf_op jit(solution)/shard_map/ppermute | solution.py:88
  36.3 29.9 %collective-permute-start.18 = (bf16[32,4864]{1,0:T(8,128)(2,1)S(1)}, bf16[32,4864]{1,0:T(8,128)(2,1)S(1)}, u32[]{:S(2)}, u32[]{:S(2)}) collective-permute-start(bf16[32,4864]{1,0:T(8,128)(2,1)S(1)} %get-tuple-element.47), channel_id=1, source_target_pairs={{0,16},{1,17},{2,18},{3,19},{4,20},{5,21},{6,22},{7,23},{8,24},{9,... | collective-permute-start | bytes 933896 | tf_op jit(solution)/shard_map/ppermute | solution.py:88
  48.5 8.3 %collective-permute-start.4 = (bf16[32,4864]{1,0:T(8,128)(2,1)S(1)}, bf16[32,4864]{1,0:T(8,128)(2,1)S(1)}, u32[]{:S(2)}, u32[]{:S(2)}) collective-permute-start(bf16[32,4864]{1,0:T(8,128)(2,1)S(1)} %get-tuple-element.55._), channel_id=1, source_target_pairs={{0,16},{1,17},{2,18},{3,19},{4,20},{5,21},{6,22},{7,23},{8,24},{9,... | collective-permute-start | bytes 933896 | tf_op jit(solution)/shard_map/ppermute | solution.py:88
  56.8 7.8 %collective-permute-start.5 = (bf16[32,4864]{1,0:T(8,128)(2,1)S(1)}, bf16[32,4864]{1,0:T(8,128)(2,1)S(1)}, u32[]{:S(2)}, u32[]{:S(2)}) collective-permute-start(bf16[32,4864]{1,0:T(8,128)(2,1)S(1)} %get-tuple-element.55._), channel_id=1, source_target_pairs={{0,24},{1,25},{2,26},{3,27},{4,28},{5,29},{6,30},{7,31},{8,16},{9,... | collective-permute-start | bytes 933896 | tf_op jit(solution)/shard_map/ppermute | solution.py:88
  66.2 12.7 %collective-permute-start.6 = (bf16[128,4864]{1,0:T(8,128)(2,1)S(1)}, bf16[128,4864]{1,0:T(8,128)(2,1)S(1)}, u32[]{:S(2)}, u32[]{:S(2)}) collective-permute-start(bf16[128,4864]{1,0:T(8,128)(2,1)S(1)} %constant_dynamic-update-slice_fusion.4.own), channel_id=1, source_target_pairs={{0,4},{1,5},{2,6},{3,7},{4,0},{5,1},{6,2},{7,3},{8,12},{9,13},{10,... | collective-permute-start | bytes 3735560 | tf_op jit(solution)/shard_map/ppermute | solution.py:88
  72.5 16.2 %collective-permute-start.20 = (bf16[128,4864]{1,0:T(8,128)(2,1)S(1)}, bf16[128,4864]{1,0:T(8,128)(2,1)S(1)}, u32[]{:S(2)}, u32[]{:S(2)}) collective-permute-start(bf16[128,4864]{1,0:T(8,128)(2,1)S(1)} %constant_dynamic-update-slice_fusion.26.refs_3_), channel_id=1, source_target_pairs={{0,4},{1,5},{2,6},{3,7},{4,0},{5,1},{6,2},{7,3},{8,12},{9,13},{10,... | collective-permute-start | bytes 3735560 | tf_op jit(solution)/shard_map/ppermute | solution.py:88
  72.6 16.0 %collective-permute-start.13 = (bf16[256,1408]{1,0:T(8,128)(2,1)S(1)}, bf16[256,1408]{1,0:T(8,128)(2,1)S(1)}, u32[]{:S(2)}, u32[]{:S(2)}) collective-permute-start(bf16[256,1408]{1,0:T(8,128)(2,1)S(1)} %constant_dynamic-update-slice_fusion.15.refs_1_), channel_id=1, source_target_pairs={{0,4},{1,5},{2,6},{3,7},{4,0},{5,1},{6,2},{7,3},{8,12},{9,13},{10,... | collective-permute-start | bytes 2162696 | tf_op jit(solution)/shard_map/ppermute | solution.py:88
  98.2 10.1 %collective-permute-start.33 = (bf16[32,1408]{1,0:T(8,128)(2,1)S(1)}, bf16[32,1408]{1,0:T(8,128)(2,1)S(1)}, u32[]{:S(2)}, u32[]{:S(2)}) collective-permute-start(bf16[32,1408]{1,0:T(8,128)(2,1)S(1)} %get-tuple-element.35), channel_id=1, source_target_pairs={{0,1},{1,0},{2,3},{3,2},{4,5},{5,4},{6,7},{7,6},{8,9},{9,8},{10,11... | collective-permute-start | bytes 270344 | tf_op jit(solution)/shard_map/ppermute | solution.py:88
  103.6 9.2 %collective-permute-start.34 = (bf16[32,1408]{1,0:T(8,128)(2,1)S(1)}, bf16[32,1408]{1,0:T(8,128)(2,1)S(1)}, u32[]{:S(2)}, u32[]{:S(2)}) collective-permute-start(bf16[32,1408]{1,0:T(8,128)(2,1)S(1)} %get-tuple-element.34), channel_id=1, source_target_pairs={{0,2},{1,3},{2,0},{3,1},{4,6},{5,7},{6,4},{7,5},{8,10},{9,11},{10,... | collective-permute-start | bytes 270344 | tf_op jit(solution)/shard_map/ppermute | solution.py:88
  103.6 9.2 %collective-permute-start.35 = (bf16[32,1408]{1,0:T(8,128)(2,1)S(1)}, bf16[32,1408]{1,0:T(8,128)(2,1)S(1)}, u32[]{:S(2)}, u32[]{:S(2)}) collective-permute-start(bf16[32,1408]{1,0:T(8,128)(2,1)S(1)} %get-tuple-element.33), channel_id=1, source_target_pairs={{0,3},{1,2},{2,1},{3,0},{4,7},{5,6},{6,5},{7,4},{8,11},{9,10},{10,... | collective-permute-start | bytes 270344 | tf_op jit(solution)/shard_map/ppermute | solution.py:88
  108.3 11.6 %collective-permute-start.21 = (bf16[128,2304]{1,0:T(8,128)(2,1)S(1)}, bf16[128,2304]{1,0:T(8,128)(2,1)S(1)}, u32[]{:S(2)}, u32[]{:S(2)}) collective-permute-start(bf16[128,2304]{1,0:T(8,128)(2,1)S(1)} %get-tuple-element.18), channel_id=1, source_target_pairs={{0,4},{1,5},{2,6},{3,7},{4,0},{5,1},{6,2},{7,3},{8,12},{9,13},{10,... | collective-permute-start | bytes 1769480 | tf_op jit(solution)/shard_map/ppermute | solution.py:88
  120.5 9.6 %collective-permute-start.23 = (bf16[32,2304]{1,0:T(8,128)(2,1)S(1)}, bf16[32,2304]{1,0:T(8,128)(2,1)S(1)}, u32[]{:S(2)}, u32[]{:S(2)}) collective-permute-start(bf16[32,2304]{1,0:T(8,128)(2,1)S(1)} %get-tuple-element.30), channel_id=1, source_target_pairs={{0,16},{1,17},{2,18},{3,19},{4,20},{5,21},{6,22},{7,23},{8,24},{9,... | collective-permute-start | bytes 442376 | tf_op jit(solution)/shard_map/ppermute | solution.py:88
  122.0 8.7 %collective-permute-start.24 = (bf16[32,2304]{1,0:T(8,128)(2,1)S(1)}, bf16[32,2304]{1,0:T(8,128)(2,1)S(1)}, u32[]{:S(2)}, u32[]{:S(2)}) collective-permute-start(bf16[32,2304]{1,0:T(8,128)(2,1)S(1)} %get-tuple-element.29), channel_id=1, source_target_pairs={{0,24},{1,25},{2,26},{3,27},{4,28},{5,29},{6,30},{7,31},{8,16},{9,... | collective-permute-start | bytes 442376 | tf_op jit(solution)/shard_map/ppermute | solution.py:88
  123.7 9.0 %collective-permute-start.26 = (bf16[32,2560]{1,0:T(8,128)(2,1)S(1)}, bf16[32,2560]{1,0:T(8,128)(2,1)S(1)}, u32[]{:S(2)}, u32[]{:S(2)}) collective-permute-start(bf16[32,2560]{1,0:T(8,128)(2,1)S(1)} %get-tuple-element.27), channel_id=1, source_target_pairs={{0,8},{1,9},{2,10},{3,11},{4,12},{5,13},{6,14},{7,15},{8,0},{9,1},... | collective-permute-start | bytes 491528 | tf_op jit(solution)/shard_map/ppermute | solution.py:88
  124.3 12.4 %collective-permute-start.27 = (bf16[32,2560]{1,0:T(8,128)(2,1)S(1)}, bf16[32,2560]{1,0:T(8,128)(2,1)S(1)}, u32[]{:S(2)}, u32[]{:S(2)}) collective-permute-start(bf16[32,2560]{1,0:T(8,128)(2,1)S(1)} %get-tuple-element.26), channel_id=1, source_target_pairs={{0,16},{1,17},{2,18},{3,19},{4,20},{5,21},{6,22},{7,23},{8,24},{9,... | collective-permute-start | bytes 491528 | tf_op jit(solution)/shard_map/ppermute | solution.py:88
  126.0 10.6 %collective-permute-start.28 = (bf16[32,2560]{1,0:T(8,128)(2,1)S(1)}, bf16[32,2560]{1,0:T(8,128)(2,1)S(1)}, u32[]{:S(2)}, u32[]{:S(2)}) collective-permute-start(bf16[32,2560]{1,0:T(8,128)(2,1)S(1)} %get-tuple-element.25), channel_id=1, source_target_pairs={{0,24},{1,25},{2,26},{3,27},{4,28},{5,29},{6,30},{7,31},{8,16},{9,... | collective-permute-start | bytes 491528 | tf_op jit(solution)/shard_map/ppermute | solution.py:88
  (20 other events, 107.1 us)

commit v2 on v1

--- a/solution.py
+++ b/solution.py
@@ -98,12 +98,17 @@
     def count(self, stage):
         return self.plane if stage == "plane" else self.blocks
 
+    def spread_out(self, array, stage):
+        others = [self.to(array, stage, k) for k in range(1, self.count(stage))]
+        return [array] + others
+
     def gather(self, array, stage):
-        others = [self.to(array, stage, k) for k in range(1, self.count(stage))]
-        return jnp.concatenate([array] + others, axis=0)
+        return jnp.concatenate(self.spread_out(array, stage), axis=0)
 
     def scatter(self, parts, stage):
-        return [parts[0]] + [self.to(parts[k], stage, k) for k in range(1, self.count(stage))]
+        return [parts[0]] + [
+            self.to(parts[k], stage, k) for k in range(1, self.count(stage))
+        ]
 
 
 def add_up(parts):
@@ -131,15 +136,45 @@
     return lax.dot_general(rows, weight, CONTRACT_LAST, preferred_element_type=F32)
 
 
-def prepare_kernel(cut, *refs):
-    tokens, out_grad, ids, gates, wide_x, wide_dy, narrow, rows_x, rows_dy, sems = refs
+def fetch(sems, *pairs):
     copies = [
-        pltpu.make_async_copy(tokens, rows_x, sems.at[0]),
-        pltpu.make_async_copy(out_grad, rows_dy, sems.at[1]),
+        pltpu.make_async_copy(source, target, sems.at[n])
+        for n, (source, target) in enumerate(pairs)
     ]
     for copy in copies:
         copy.start()
-    tok, width = rows_x.shape
+    return copies
+
+
+def wide_kernel(cut, tokens, out_grad, wide_x, wide_dy, sems):
+    for copy in fetch(
+        sems, (tokens.at[:, :cut], wide_x), (out_grad.at[:, :cut], wide_dy)
+    ):
+        copy.wait()
+
+
+def wide_part(tokens, out_grad, cut):
+    wide = jax.ShapeDtypeStruct((tokens.shape[0], cut), BF16)
+    return pl.pallas_call(
+        functools.partial(wide_kernel, cut),
+        out_shape=(wide, wide),
+        in_specs=[HBM, HBM],
+        out_specs=(VMEM, VMEM),
+        scratch_shapes=[pltpu.SemaphoreType.DMA((2,))],
+        compiler_params=params(2),
+        cost_estimate=pl.CostEstimate(
+            flops=20000000000, bytes_accessed=40000000, transcendentals=0
+        ),
+    )(tokens, out_grad)
+
+
+def narrow_kernel(cut, tokens, out_grad, ids, gates, narrow, sems):
+    tok, width = tokens.shape
+    copies = fetch(
+        sems,
+        (tokens.at[:, cut:], narrow.at[:tok, : width - cut]),
+        (out_grad.at[:, cut:], narrow.at[tok:, : width - cut]),
+    )
     expert = lax.broadcasted_iota(jnp.int32, (LANES, tok), 0)
     table = jnp.zeros((LANES, tok), F32)
     for k in range(ids.shape[0]):
@@ -147,98 +182,101 @@
         table = table + jnp.where(expert == ids[k : k + 1, :], gate, 0.0)
     narrow[:tok, width - cut :] = jnp.zeros((tok, LANES), BF16)
     narrow[tok:, width - cut :] = table.T.astype(BF16)
-    copies[0].wait()
-    wide_x[...] = rows_x[:, :cut]
-    narrow[:tok, : width - cut] = rows_x[:, cut:]
-    copies[1].wait()
-    wide_dy[...] = rows_dy[:, :cut]
-    narrow[tok:, : width - cut] = rows_dy[:, cut:]
-
-
-def prepare(tokens, out_grad, ids, gates, cut):
+    for copy in copies:
+        copy.wait()
+
+
+def narrow_part(tokens, out_grad, ids, gates, cut):
     tok, width = tokens.shape
-    wide = jax.ShapeDtypeStruct((tok, cut), BF16)
-    return pl.pallas_call(
-        functools.partial(prepare_kernel, cut),
-        out_shape=(wide, wide, jax.ShapeDtypeStruct((2 * tok, width - cut + LANES), BF16)),
+    return pl.pallas_call(
+        functools.partial(narrow_kernel, cut),
+        out_shape=jax.ShapeDtypeStruct((2 * tok, width - cut + LANES), BF16),
         in_specs=[HBM, HBM, VMEM, VMEM],
-        out_specs=(VMEM,) * 3,
-        scratch_shapes=[pltpu.VMEM((tok, width), BF16)] * 2
-        + [pltpu.SemaphoreType.DMA((2,))],
+        out_specs=VMEM,
+        scratch_shapes=[pltpu.SemaphoreType.DMA((2,))],
         compiler_params=params(2),
-    )(in_hbm(tokens), in_hbm(out_grad), ids.T, gates.T)
+    )(tokens, out_grad, ids.T, gates.T)
 
 
 def in_hbm(array):
     return pltpu.with_memory_space_constraint(array, pltpu.HBM)
 
 
-def stack(own, other, rows):
-    half = own.shape[0]
-    rows[:half, :] = own[...]
-    rows[half:, :] = other[...]
-
-
-def load_kernel(source, _, held, sem):
-    copy = pltpu.make_async_copy(source, held, sem)
-    copy.start()
-    copy.wait()
-
-
-def load(weight, after, grant):
-    return pl.pallas_call(
-        load_kernel,
-        out_shape=jax.ShapeDtypeStruct(weight.shape, BF16),
-        in_specs=[HBM, pl.BlockSpec(memory_space=pl.ANY)],
-        out_specs=VMEM,
-        scratch_shapes=[pltpu.SemaphoreType.DMA],
-        compiler_params=params(grant),
-        cost_estimate=cost(0, *weight.shape),
-    )(weight, after)
-
-
-def first_kernel(own, other, weight, pre, rows):
-    width = own.shape[1]
-    stack(own, other, rows)
+def stack(blocks, rows):
+    step = blocks[0].shape[0]
+    for n, block in enumerate(blocks):
+        rows[n * step : (n + 1) * step, :] = block[...]
+
+
+def first_kernel(*refs):
+    *blocks, weight, pre, rows = refs
+    stack(blocks, rows)
+    width = rows.shape[1]
     for at, to in column_blocks(weight.shape[0]):
         pre[:, at:to] = times(rows[...], weight[at:to, :width])
 
 
-def first_product(own, other, weight):
-    half, width = own.shape
-    hidden = weight.shape[0]
+def first_product(blocks, weight):
+    step, width = blocks[0].shape
+    rows, hidden = step * len(blocks), weight.shape[0]
     return pl.pallas_call(
         first_kernel,
-        out_shape=jax.ShapeDtypeStruct((2 * half, hidden), F32),
-        in_specs=[VMEM, VMEM, VMEM],
+        out_shape=jax.ShapeDtypeStruct((rows, hidden), F32),
+        in_specs=[VMEM] * (len(blocks) + 1),
         out_specs=VMEM,
-        scratch_shapes=[pltpu.VMEM((2 * half, width), BF16)],
-        compiler_params=params(LAST_GRANT),
-        cost_estimate=cost(2 * half, hidden, width),
-    )(own, other, weight)
-
-
-def last_kernel(plane, blocks, tok, *refs):
-    pre_ref, n_own, n_other, own, other, weight_in, weight_down = refs[:7]
-    slope_ref, part_ref, rows, rows_x, rows_dy, table = refs[7:]
-    cut, rest = rows.shape[1], rows_x.shape[1]
-    stack(own, other, rows)
-    for c, ref in enumerate((n_own, n_other)):
+        scratch_shapes=[pltpu.VMEM((rows, width), BF16)],
+        compiler_params=params(SMALL_GRANT),
+        cost_estimate=cost(rows, hidden, width),
+    )(*blocks, weight)
+
+
+def unpack(plane, blocks, tok, offset, sources, columns, rows):
+    for c, ref in enumerate(sources):
         for z in range(blocks):
             for p in range(plane):
-                at = (z * plane + p) * 2 * tok
+                at = (z * plane + p) * 2 * tok + offset
                 to = ((c * plane + p) * blocks + z) * tok
-                rows_x[to : to + tok, :] = ref[at : at + tok, :rest]
-                rows_dy[to : to + tok, :] = ref[at + tok : at + 2 * tok, :rest]
-                table[to : to + tok, :] = ref[at + tok : at + 2 * tok, rest:].astype(F32)
+                rows[to : to + tok, :] = ref[at : at + tok, columns].astype(rows.dtype)
+
+
+def middle_kernel(plane, blocks, tok, cut, *refs):
+    pre, n_own, n_other, weight, pre_out, rows = refs
+    width = rows.shape[1]
+    unpack(plane, blocks, tok, 0, (n_own, n_other), slice(0, width), rows)
+    for at, to in column_blocks(weight.shape[0]):
+        pre_out[:, at:to] = pre[:, at:to] + times(rows[...], weight[at:to, cut:])
+
+
+def middle_product(pre, n_own, n_other, weight, cut, ring, tok):
+    rows, hidden = pre.shape
+    width = weight.shape[1] - cut
+    return pl.pallas_call(
+        functools.partial(middle_kernel, ring.plane, ring.blocks, tok, cut),
+        out_shape=jax.ShapeDtypeStruct((rows, hidden), F32),
+        in_specs=[VMEM] * 4,
+        out_specs=VMEM,
+        scratch_shapes=[pltpu.VMEM((rows, width), BF16)],
+        input_output_aliases={0: 0},
+        compiler_params=params(SMALL_GRANT),
+        cost_estimate=cost(rows, hidden, width),
+    )(pre, n_own, n_other, weight)
+
+
+def last_kernel(plane, blocks, tok, *refs):
+    pre_ref, n_own, n_other, *own, weight, slope_ref, part_ref, rows, rest, table = refs
+    stack(own, rows)
+    cut, width = rows.shape[1], rest.shape[1]
+    narrow = (n_own, n_other)
+    unpack(plane, blocks, tok, tok, narrow, slice(0, width), rest)
+    unpack(plane, blocks, tok, tok, narrow, slice(width, width + LANES), table)
     lane = lax.broadcasted_iota(jnp.int32, (1, LANES), 1)
     mask = (lane == lax.axis_index("expert")).astype(F32)
     gate = jnp.sum(table[...] * mask, axis=1, keepdims=True)
     total = jnp.zeros((rows.shape[0], 1), F32)
-    for at, to in column_blocks(weight_in.shape[0]):
-        pre = pre_ref[:, at:to] + times(rows_x[...], weight_in[at:to, cut:])
-        back = times(rows_dy[...], weight_down[at:to, cut:])
-        back = back + times(rows[...], weight_down[at:to, :cut])
+    for at, to in column_blocks(weight.shape[0]):
+        pre = pre_ref[:, at:to]
+        back = times(rest[...], weight[at:to, cut:])
+        back = back + times(rows[...], weight[at:to, :cut])
         sigma = jax.nn.sigmoid(pre)
         total = total + jnp.sum(pre * sigma * back, axis=1, keepdims=True)
         slope = gate * back * sigma * (1.0 + pre * (1.0 - sigma))
@@ -246,27 +284,25 @@
     part_ref[...] = (total * mask).astype(BF16)
 
 
-def last_product(pre, n_own, n_other, own, other, weight_in, weight_down, ring, tok):
+def last_product(pre, n_own, n_other, blocks, weight, ring, tok):
     rows, hidden = pre.shape
-    width = weight_in.shape[1]
-    cut = own.shape[1]
+    width, cut = weight.shape[1], blocks[0].shape[1]
     return pl.pallas_call(
         functools.partial(last_kernel, ring.plane, ring.blocks, tok),
         out_shape=(
             jax.ShapeDtypeStruct((rows, hidden), BF16),
             jax.ShapeDtypeStruct((rows, LANES), BF16),
         ),
-        in_specs=[VMEM] * 7,
+        in_specs=[VMEM] * (len(blocks) + 4),
         out_specs=(VMEM, VMEM),
         scratch_shapes=[
             pltpu.VMEM((rows, cut), BF16),
             pltpu.VMEM((rows, width - cut), BF16),
-            pltpu.VMEM((rows, width - cut), BF16),
             pltpu.VMEM((rows, LANES), F32),
         ],
-        compiler_params=params(LAST_GRANT),
-        cost_estimate=cost(rows, hidden, 2 * width - cut),
-    )(pre, n_own, n_other, own, other, weight_in, weight_down)
+        compiler_params=params(SMALL_GRANT),
+        cost_estimate=cost(rows, hidden, width),
+    )(pre, n_own, n_other, *blocks, weight)
 
 
 def spread_kernel(lo, hi, *refs):
@@ -319,25 +355,30 @@
     ring = Ring(lax.axis_size("expert"), lax.axis_size("blk"))
     cut = cut_of(width)
     lanes = jnp.arange(LANES, dtype=jnp.int32)
-    weight_in, weight_down = in_hbm(w_in[0]), in_hbm(w_down[0])
-    wide_x, wide_dy, narrow = prepare(tokens, out_grad, expert_ids, gates, cut)
+    held_in, held_down = w_in[0], w_down[0]
+    unchosen = (expert_ids[:, :, None] != lanes[None, None, :]).astype(F32)
+    unchosen = lax.optimization_barrier(unchosen)
+    tokens, out_grad = in_hbm(tokens), in_hbm(out_grad)
+    wide_x, wide_dy = wide_part(tokens, out_grad, cut)
     x_line = ring.gather(wide_x, "line")
+    narrow = narrow_part(tokens, out_grad, expert_ids, gates, cut)
     n_plane = ring.gather(narrow, "plane")
-    x_own = ring.gather(x_line, "plane")
+    x_own = ring.spread_out(x_line, "plane")
     dy_line = ring.gather(wide_dy, "line")
     n_own = ring.gather(n_plane, "line")
-    dy_own = ring.gather(dy_line, "plane")
-    held_in = load(weight_in, x_line, LOAD_GRANT)
-    x_other = ring.core(x_own)
-    pre = first_product(x_own, x_other, held_in)
-    held_down = load(weight_down, pre, DOWN_GRANT)
+    dy_own = ring.spread_out(dy_line, "plane")
+    x_other = [ring.core(block) for block in x_own]
+    pre = first_product(x_own + x_other, held_in)
     n_other = ring.core(n_own)
-    dy_other = ring.core(dy_own)
-    slope, part = last_product(pre, n_own, n_other, dy_own, dy_other, held_in, held_down, ring, tok)
-
-    chosen = (expert_ids[:, :, None] == lanes[None, None, :]).astype(F32)
-    chosen = lax.optimization_barrier(chosen)
-    mid = cut // 2 // 256 * 256
+    pre = middle_product(pre, n_own, n_other, held_in, cut, ring, tok)
+    dy_other = [ring.core(block) for block in dy_own]
+    slope, part = last_product(
+        pre, n_own, n_other, dy_own + dy_other, held_down, ring, tok
+    )
+
+    chosen = lax.optimization_barrier(1.0 - unchosen)
+    unchosen = lax.optimization_barrier(1.0 - chosen)
+    mid, cut = width * 10 // 24, width * 19 // 24
     own1, other1 = spread(slope, held_in, 0, mid, ())
     own2, other2 = spread(slope, held_in, mid, cut, ())
     own3, other3 = spread(slope, held_in, cut, width, (part,))
@@ -352,18 +393,16 @@
     sum_wide = add_up(ring.scatter(wide, "line"))
     sum_rest = add_up(ring.scatter(rest, "plane"))
     grad_tokens = jnp.concatenate([sum_wide, sum_rest[:, : width - cut]], axis=1)
-    grad_gates = jnp.sum(chosen * sum_rest[:, None, width - cut :], axis=2)
+    grad_gates = jnp.sum((1.0 - unchosen) * sum_rest[:, None, width - cut :], axis=2)
     return grad_tokens.astype(BF16), grad_gates.astype(BF16)
 
 
 def cut_of(width):
-    return width * 19 // 24 // 256 * 256
+    return width * 18 // 24 // 256 * 256
 
 
 GRANT = 8
-LOAD_GRANT = 4
-DOWN_GRANT = 4
-LAST_GRANT = 8
+SMALL_GRANT = 8
 
 
 def power_of_two(n):

time: 147 us -> 122 us (0.83)
  waiting for transfers between devices: 59.5 us -> 48.1 us
  Pallas kernels: 28.2 us -> 18.3 us
  starting transfers between devices: 54.4 us -> 50.6 us
    ppermute x39 -> x45, waiting for transfers between devices: 59.5 us -> 48.1 us  [move(): return lax.ppermute(array, AXES, pairs)]
    pallas_call x4, Pallas kernels: 16.4 us -> 7.35 us  [the longest x1 3.88 us: first_product(): pl.pallas_call(first_kernel, out_shape=jax.ShapeDtypeStruct((rows, hidden...]
    ppermute x39 -> x45, starting transfers between devices: 54.4 us -> 50.6 us  [move(): return lax.ppermute(array, AXES, pairs)]
  transfers between devices with their start and end apart: 39 -> 45, of which waited for: 19 -> 16; matrix products, arithmetic and copies ran while one was open for 1% -> 1% of each run, Pallas kernels for 13% -> 9%
where the time goes in v2:
time: 122 us
  starting transfers between devices  50.6 us (41%)
  waiting for transfers between devices  48.1 us (39%)
  Pallas kernels  18.3 us (15%)
  other arithmetic  2.07 us (2%)
  local copies, waits for them, and re-layouts  1.87 us (2%)
    ppermute x45, starting transfers between devices, move(): return lax.ppermute(array, AXES, pairs)  50.6 us
    ppermute x45, waiting for transfers between devices, move(): return lax.ppermute(array, AXES, pairs)  48.1 us
    pallas_call x3, Pallas kernels, spread(): pl.pallas_call(functools.partial(spread_kernel, lo, hi), out_shape=(half,...  5.57 us
    pallas_call x1, Pallas kernels, last_product(): pl.pallas_call(functools.partial(last_kernel, ring.plane, ring.blocks, to...  5.41 us
    pallas_call x1, Pallas kernels, first_product(): pl.pallas_call(first_kernel, out_shape=jax.ShapeDtypeStruct((rows, hidden...  3.88 us
  transfers between devices with their start and end apart: 45, of which 16 were waited for; matrix products, arithmetic and copies ran while one was open for 1% of the time, Pallas kernels for 9%

profile of v2, /device:TPU:0, one launch (start us, length us, event | category | flops | bytes accessed | tf_op | source)
XLA Modules:
  0.0 121.9 jit_solution(5606225856279376115)
XLA Ops:
  1.8 3.1 %collective-permute-start = (bf16[8,4608]{1,0:T(8,128)(2,1)S(1)}, bf16[8,4608]{1,0:T(8,128)(2,1)S(1)}, u32[]{:S(2)}, u32[]{:S(2)}) collective-permute-start(bf16[8,4608]{1,0:T(8,128)(2,1)S(1)} %get-tuple-element.12), channel_id=1, source_target_pairs={{0,1},{1,0},{2,3},{3,2},{4,5},{5,4},{6,7},{7,6},{8,9},{9,8},{10,11... | collective-permute-start | bytes 221192 | tf_op jit(solution)/shard_map/ppermute | solution.py:88
  4.9 2.6 %collective-permute-start.1 = (bf16[8,4608]{1,0:T(8,128)(2,1)S(1)}, bf16[8,4608]{1,0:T(8,128)(2,1)S(1)}, u32[]{:S(2)}, u32[]{:S(2)}) collective-permute-start(bf16[8,4608]{1,0:T(8,128)(2,1)S(1)} %get-tuple-element.12), channel_id=1, source_target_pairs={{0,2},{1,3},{2,0},{3,1},{4,6},{5,7},{6,4},{7,5},{8,10},{9,11},{10,... | collective-permute-start | bytes 221192 | tf_op jit(solution)/shard_map/ppermute | solution.py:88
  12.5 2.7 %collective-permute-start.12 = (bf16[16,1664]{1,0:T(8,128)(2,1)S(1)}, bf16[16,1664]{1,0:T(8,128)(2,1)S(1)}, u32[]{:S(2)}, u32[]{:S(2)}) collective-permute-start(bf16[16,1664]{1,0:T(8,128)(2,1)S(1)} %shard_map.79), channel_id=1, source_target_pairs={{0,24},{1,25},{2,26},{3,27},{4,28},{5,29},{6,30},{7,31},{8,16},{9,... | collective-permute-start | bytes 159752 | tf_op jit(solution)/shard_map/ppermute | solution.py:88
  17.5 2.0 %collective-permute-start.18 = (bf16[8,4608]{1,0:T(8,128)(2,1)S(1)}, bf16[8,4608]{1,0:T(8,128)(2,1)S(1)}, u32[]{:S(2)}, u32[]{:S(2)}) collective-permute-start(bf16[8,4608]{1,0:T(8,128)(2,1)S(1)} %get-tuple-element.13), channel_id=1, source_target_pairs={{0,2},{1,3},{2,0},{3,1},{4,6},{5,7},{6,4},{7,5},{8,10},{9,11},{10,... | collective-permute-start | bytes 221192 | tf_op jit(solution)/shard_map/ppermute | solution.py:88
  19.6 1.9 %collective-permute-start.19 = (bf16[8,4608]{1,0:T(8,128)(2,1)S(1)}, bf16[8,4608]{1,0:T(8,128)(2,1)S(1)}, u32[]{:S(2)}, u32[]{:S(2)}) collective-permute-start(bf16[8,4608]{1,0:T(8,128)(2,1)S(1)} %get-tuple-element.13), channel_id=1, source_target_pairs={{0,3},{1,2},{2,1},{3,0},{4,7},{5,6},{6,5},{7,4},{8,11},{9,10},{10,... | collective-permute-start | bytes 221192 | tf_op jit(solution)/shard_map/ppermute | solution.py:88
  22.1 2.1 %collective-permute-start.14 = (bf16[64,1664]{1,0:T(8,128)(2,1)S(1)}, bf16[64,1664]{1,0:T(8,128)(2,1)S(1)}, u32[]{:S(2)}, u32[]{:S(2)}) collective-permute-start(bf16[64,1664]{1,0:T(8,128)(2,1)S(1)} %pad_maximum_fusion), channel_id=1, source_target_pairs={{0,2},{1,3},{2,0},{3,1},{4,6},{5,7},{6,4},{7,5},{8,10},{9,11},{10,... | collective-permute-start | bytes 638984 | tf_op jit(solution)/shard_map/ppermute | solution.py:88
  29.8 2.4 %collective-permute-start.5 = (bf16[32,4608]{1,0:T(8,128)(2,1)S(1)}, bf16[32,4608]{1,0:T(8,128)(2,1)S(1)}, u32[]{:S(2)}, u32[]{:S(2)}) collective-permute-start(bf16[32,4608]{1,0:T(8,128)(2,1)S(1)} %constant_dynamic-update-slice_fusion.refs_0_), channel_id=1, source_target_pairs={{0,24},{1,25},{2,26},{3,27},{4,28},{5,29},{6,30},{7,31},{8,16},{9,... | collective-permute-start | bytes 884744 | tf_op jit(solution)/shard_map/ppermute | solution.py:88
  32.3 8.7 %collective-permute-done.14 = bf16[64,1664]{1,0:T(8,128)(2,1)S(1)} collective-permute-done((bf16[64,1664]{1,0:T(8,128)(2,1)S(1)}, bf16[64,1664]{1,0:T(8,128)(2,1)S(1)}, u32[]{:S(2)}, u32[]{:S(2)}) %collective-permute-start.14) | collective-permute-done | bytes 213024 | tf_op jit(solution)/shard_map/ppermute | solution.py:88
  45.0 6.1 %collective-permute-done.20.refs_4_ = bf16[32,4608]{1,0:T(8,128)(2,1)S(1)} collective-permute-done((bf16[32,4608]{1,0:T(8,128)(2,1)S(1)}, bf16[32,4608]{1,0:T(8,128)(2,1)S(1)}, u32[]{:S(2)}, u32[]{:S(2)}) %collective-permute-start.20) | collective-permute-done | bytes 294944 | tf_op jit(solution)/shard_map/ppermute | solution.py:88
  51.0 7.1 %collective-permute-done.21.refs_5_ = bf16[32,4608]{1,0:T(8,128)(2,1)S(1)} collective-permute-done((bf16[32,4608]{1,0:T(8,128)(2,1)S(1)}, bf16[32,4608]{1,0:T(8,128)(2,1)S(1)}, u32[]{:S(2)}, u32[]{:S(2)}) %collective-permute-start.21) | collective-permute-done | bytes 294944 | tf_op jit(solution)/shard_map/ppermute | solution.py:88
  59.8 3.9 %shard_map.78.refs_0_ = f32[256,1344]{1,0:T(8,128)S(1)} custom-call(bf16[32,4608]{1,0:T(8,128)(2,1)S(1)} %constant_dynamic-update-slice_fusion.refs_0_, bf16[32,4608]{1,0:T(8,128)(2,1)S(1)} %collective-permute-done.3.refs_1_, bf16[32,4608]{1,0:T(8,128)(2,1)S(1)} %collective-permute-done.4.refs_2_, bf16[32,4608]{1,0:T(8,128)(2,1)S(1)} %collective-permute-done.5.refs_3_, ...), custom_call_target="tpu_custom_call" | custom-call | flops 3170893824 | bytes 12386304 | tf_op jit(solution)/shard_map/pallas_call | solution.py:222
  67.1 5.4 %shard_map.81 = (bf16[256,1344]{1,0:T(8,128)(2,1)S(1)}, bf16[256,128]{1,0:T(8,128)(2,1)S(1)}) custom-call(f32[256,1344]{1,0:T(8,128)S(1)} %shard_map.80.refs_0_, bf16[256,1664]{1,0:T(8,128)(2,1)S(1)} %constant_dynamic-update-slice_fusion.4.refs_1_, bf16[256,1664]{1,0:T(8,128)(2,1)S(1)} %collective-permute-done.16.refs_2_, ...), custom_call_target="tpu_custom_call" | custom-call | flops 4227858432 | bytes 16515072 | tf_op jit(solution)/shard_map/pallas_call | solution.py:290
  76.8 2.3 %collective-permute-start.40 = (bf16[32,1408]{1,0:T(8,128)(2,1)S(1)}, bf16[32,1408]{1,0:T(8,128)(2,1)S(1)}, u32[]{:S(2)}, u32[]{:S(2)}) collective-permute-start(bf16[32,1408]{1,0:T(8,128)(2,1)S(1)} %get-tuple-element.32), channel_id=1, source_target_pairs={{0,2},{1,3},{2,0},{3,1},{4,6},{5,7},{6,4},{7,5},{8,10},{9,11},{10,... | collective-permute-start | bytes 270344 | tf_op jit(solution)/shard_map/ppermute | solution.py:88
  80.2 2.0 %shard_map.83 = (bf16[128,2304]{1,0:T(8,128)(2,1)S(1)}, bf16[128,2304]{1,0:T(8,128)(2,1)S(1)}) custom-call(bf16[256,1344]{1,0:T(8,128)(2,1)S(1)} %get-tuple-element.14.refs_0_, bf16[1344,6144]{1,0:T(8,128)(2,1)S(1)} %bitcast.79), custom_call_target="tpu_custom_call" | custom-call | flops 1585446912 | bytes 6193152 | tf_op jit(solution)/shard_map/pallas_call | solution.py:325
  82.6 4.2 %collective-permute-done.41 = bf16[32,1408]{1,0:T(8,128)(2,1)S(1)} collective-permute-done((bf16[32,1408]{1,0:T(8,128)(2,1)S(1)}, bf16[32,1408]{1,0:T(8,128)(2,1)S(1)}, u32[]{:S(2)}, u32[]{:S(2)}) %collective-permute-start.41) | collective-permute-done | bytes 90144 | tf_op jit(solution)/shard_map/ppermute | solution.py:88
  90.4 2.2 %shard_map.82 = (bf16[128,2560]{1,0:T(8,128)(2,1)S(1)}, bf16[128,2560]{1,0:T(8,128)(2,1)S(1)}) custom-call(bf16[256,1344]{1,0:T(8,128)(2,1)S(1)} %get-tuple-element.14.refs_0_, bf16[1344,6144]{1,0:T(8,128)(2,1)S(1)} %bitcast.80), custom_call_target="tpu_custom_call" | custom-call | flops 1761607680 | bytes 6881280 | tf_op jit(solution)/shard_map/pallas_call | solution.py:325
  92.7 1.9 %collective-permute-done.44 = bf16[8,1408]{1,0:T(8,128)(2,1)S(1)} collective-permute-done((bf16[8,1408]{1,0:T(8,128)(2,1)S(1)}, bf16[8,1408]{1,0:T(8,128)(2,1)S(1)}, u32[]{:S(2)}, u32[]{:S(2)}) %collective-permute-start.44) | collective-permute-done | bytes 22560 | tf_op jit(solution)/shard_map/ppermute | solution.py:88
  96.0 2.4 %collective-permute-start.34 = (bf16[32,2304]{1,0:T(8,128)(2,1)S(1)}, bf16[32,2304]{1,0:T(8,128)(2,1)S(1)}, u32[]{:S(2)}, u32[]{:S(2)}) collective-permute-start(bf16[32,2304]{1,0:T(8,128)(2,1)S(1)} %get-tuple-element.27), channel_id=1, source_target_pairs={{0,24},{1,25},{2,26},{3,27},{4,28},{5,29},{6,30},{7,31},{8,16},{9,... | collective-permute-start | bytes 442376 | tf_op jit(solution)/shard_map/ppermute | solution.py:88
  99.7 1.9 %collective-permute-done.32 = bf16[32,2304]{1,0:T(8,128)(2,1)S(1)} collective-permute-done((bf16[32,2304]{1,0:T(8,128)(2,1)S(1)}, bf16[32,2304]{1,0:T(8,128)(2,1)S(1)}, u32[]{:S(2)}, u32[]{:S(2)}) %collective-permute-start.32) | collective-permute-done | bytes 147488 | tf_op jit(solution)/shard_map/ppermute | solution.py:88
  102.2 2.4 %collective-permute-done.33 = bf16[32,2304]{1,0:T(8,128)(2,1)S(1)} collective-permute-done((bf16[32,2304]{1,0:T(8,128)(2,1)S(1)}, bf16[32,2304]{1,0:T(8,128)(2,1)S(1)}, u32[]{:S(2)}, u32[]{:S(2)}) %collective-permute-start.33) | collective-permute-done | bytes 147488 | tf_op jit(solution)/shard_map/ppermute | solution.py:88
  104.6 3.7 %collective-permute-done.28 = bf16[32,2560]{1,0:T(8,128)(2,1)S(1)} collective-permute-done((bf16[32,2560]{1,0:T(8,128)(2,1)S(1)}, bf16[32,2560]{1,0:T(8,128)(2,1)S(1)}, u32[]{:S(2)}, u32[]{:S(2)}) %collective-permute-start.28) | collective-permute-done | bytes 163872 | tf_op jit(solution)/shard_map/ppermute | solution.py:88
  108.3 2.5 %collective-permute-done.29 = bf16[32,2560]{1,0:T(8,128)(2,1)S(1)} collective-permute-done((bf16[32,2560]{1,0:T(8,128)(2,1)S(1)}, bf16[32,2560]{1,0:T(8,128)(2,1)S(1)}, u32[]{:S(2)}, u32[]{:S(2)}) %collective-permute-start.29) | collective-permute-done | bytes 163872 | tf_op jit(solution)/shard_map/ppermute | solution.py:88
  110.9 1.9 %collective-permute-start.35 = (bf16[8,4864]{1,0:T(8,128)(2,1)S(1)}, bf16[8,4864]{1,0:T(8,128)(2,1)S(1)}, u32[]{:S(2)}, u32[]{:S(2)}) collective-permute-start(bf16[8,4864]{1,0:T(8,128)(2,1)S(1)} %pad_maximum_fusion.2), channel_id=1, source_target_pairs={{0,1},{1,0},{2,3},{3,2},{4,5},{5,4},{6,7},{7,6},{8,9},{9,8},{10,11... | collective-permute-start | bytes 233480 | tf_op jit(solution)/shard_map/ppermute | solution.py:88
  116.7 4.5 %collective-permute-done.36 = bf16[8,4864]{1,0:T(8,128)(2,1)S(1)} collective-permute-done((bf16[8,4864]{1,0:T(8,128)(2,1)S(1)}, bf16[8,4864]{1,0:T(8,128)(2,1)S(1)}, u32[]{:S(2)}, u32[]{:S(2)}) %collective-permute-start.36) | collective-permute-done | bytes 77856 | tf_op jit(solution)/shard_map/ppermute | solution.py:88
  (123 shorter events, 41.2 us)
Async XLA Ops:
  1.8 17.8 %collective-permute-start = (bf16[8,4608]{1,0:T(8,128)(2,1)S(1)}, bf16[8,4608]{1,0:T(8,128)(2,1)S(1)}, u32[]{:S(2)}, u32[]{:S(2)}) collective-permute-start(bf16[8,4608]{1,0:T(8,128)(2,1)S(1)} %get-tuple-element.12), channel_id=1, source_target_pairs={{0,1},{1,0},{2,3},{3,2},{4,5},{5,4},{6,7},{7,6},{8,9},{9,8},{10,11... | collective-permute-start | bytes 221192 | tf_op jit(solution)/shard_map/ppermute | solution.py:88
  4.9 16.6 %collective-permute-start.1 = (bf16[8,4608]{1,0:T(8,128)(2,1)S(1)}, bf16[8,4608]{1,0:T(8,128)(2,1)S(1)}, u32[]{:S(2)}, u32[]{:S(2)}) collective-permute-start(bf16[8,4608]{1,0:T(8,128)(2,1)S(1)} %get-tuple-element.12), channel_id=1, source_target_pairs={{0,2},{1,3},{2,0},{3,1},{4,6},{5,7},{6,4},{7,5},{8,10},{9,11},{10,... | collective-permute-start | bytes 221192 | tf_op jit(solution)/shard_map/ppermute | solution.py:88
  7.5 14.7 %collective-permute-start.2 = (bf16[8,4608]{1,0:T(8,128)(2,1)S(1)}, bf16[8,4608]{1,0:T(8,128)(2,1)S(1)}, u32[]{:S(2)}, u32[]{:S(2)}) collective-permute-start(bf16[8,4608]{1,0:T(8,128)(2,1)S(1)} %get-tuple-element.12), channel_id=1, source_target_pairs={{0,3},{1,2},{2,1},{3,0},{4,7},{5,6},{6,5},{7,4},{8,11},{9,10},{10,... | collective-permute-start | bytes 221192 | tf_op jit(solution)/shard_map/ppermute | solution.py:88
  15.1 9.1 %collective-permute-start.17 = (bf16[8,4608]{1,0:T(8,128)(2,1)S(1)}, bf16[8,4608]{1,0:T(8,128)(2,1)S(1)}, u32[]{:S(2)}, u32[]{:S(2)}) collective-permute-start(bf16[8,4608]{1,0:T(8,128)(2,1)S(1)} %get-tuple-element.13), channel_id=1, source_target_pairs={{0,1},{1,0},{2,3},{3,2},{4,5},{5,4},{6,7},{7,6},{8,9},{9,8},{10,11... | collective-permute-start | bytes 221192 | tf_op jit(solution)/shard_map/ppermute | solution.py:88
  17.5 8.6 %collective-permute-start.18 = (bf16[8,4608]{1,0:T(8,128)(2,1)S(1)}, bf16[8,4608]{1,0:T(8,128)(2,1)S(1)}, u32[]{:S(2)}, u32[]{:S(2)}) collective-permute-start(bf16[8,4608]{1,0:T(8,128)(2,1)S(1)} %get-tuple-element.13), channel_id=1, source_target_pairs={{0,2},{1,3},{2,0},{3,1},{4,6},{5,7},{6,4},{7,5},{8,10},{9,11},{10,... | collective-permute-start | bytes 221192 | tf_op jit(solution)/shard_map/ppermute | solution.py:88
  19.6 8.1 %collective-permute-start.19 = (bf16[8,4608]{1,0:T(8,128)(2,1)S(1)}, bf16[8,4608]{1,0:T(8,128)(2,1)S(1)}, u32[]{:S(2)}, u32[]{:S(2)}) collective-permute-start(bf16[8,4608]{1,0:T(8,128)(2,1)S(1)} %get-tuple-element.13), channel_id=1, source_target_pairs={{0,3},{1,2},{2,1},{3,0},{4,7},{5,6},{6,5},{7,4},{8,11},{9,10},{10,... | collective-permute-start | bytes 221192 | tf_op jit(solution)/shard_map/ppermute | solution.py:88
  21.5 8.4 %collective-permute-start.13 = (bf16[64,1664]{1,0:T(8,128)(2,1)S(1)}, bf16[64,1664]{1,0:T(8,128)(2,1)S(1)}, u32[]{:S(2)}, u32[]{:S(2)}) collective-permute-start(bf16[64,1664]{1,0:T(8,128)(2,1)S(1)} %pad_maximum_fusion), channel_id=1, source_target_pairs={{0,1},{1,0},{2,3},{3,2},{4,5},{5,4},{6,7},{7,6},{8,9},{9,8},{10,11... | collective-permute-start | bytes 638984 | tf_op jit(solution)/shard_map/ppermute | solution.py:88
  22.1 18.9 %collective-permute-start.14 = (bf16[64,1664]{1,0:T(8,128)(2,1)S(1)}, bf16[64,1664]{1,0:T(8,128)(2,1)S(1)}, u32[]{:S(2)}, u32[]{:S(2)}) collective-permute-start(bf16[64,1664]{1,0:T(8,128)(2,1)S(1)} %pad_maximum_fusion), channel_id=1, source_target_pairs={{0,2},{1,3},{2,0},{3,1},{4,6},{5,7},{6,4},{7,5},{8,10},{9,11},{10,... | collective-permute-start | bytes 638984 | tf_op jit(solution)/shard_map/ppermute | solution.py:88
  24.2 16.9 %collective-permute-start.15 = (bf16[64,1664]{1,0:T(8,128)(2,1)S(1)}, bf16[64,1664]{1,0:T(8,128)(2,1)S(1)}, u32[]{:S(2)}, u32[]{:S(2)}) collective-permute-start(bf16[64,1664]{1,0:T(8,128)(2,1)S(1)} %pad_maximum_fusion), channel_id=1, source_target_pairs={{0,3},{1,2},{2,1},{3,0},{4,7},{5,6},{6,5},{7,4},{8,11},{9,10},{10,... | collective-permute-start | bytes 638984 | tf_op jit(solution)/shard_map/ppermute | solution.py:88
  26.1 16.6 %collective-permute-start.3 = (bf16[32,4608]{1,0:T(8,128)(2,1)S(1)}, bf16[32,4608]{1,0:T(8,128)(2,1)S(1)}, u32[]{:S(2)}, u32[]{:S(2)}) collective-permute-start(bf16[32,4608]{1,0:T(8,128)(2,1)S(1)} %constant_dynamic-update-slice_fusion.refs_0_), channel_id=1, source_target_pairs={{0,8},{1,9},{2,10},{3,11},{4,12},{5,13},{6,14},{7,15},{8,0},{9,1},... | collective-permute-start | bytes 884744 | tf_op jit(solution)/shard_map/ppermute | solution.py:88
  27.6 16.6 %collective-permute-start.4 = (bf16[32,4608]{1,0:T(8,128)(2,1)S(1)}, bf16[32,4608]{1,0:T(8,128)(2,1)S(1)}, u32[]{:S(2)}, u32[]{:S(2)}) collective-permute-start(bf16[32,4608]{1,0:T(8,128)(2,1)S(1)} %constant_dynamic-update-slice_fusion.refs_0_), channel_id=1, source_target_pairs={{0,16},{1,17},{2,18},{3,19},{4,20},{5,21},{6,22},{7,23},{8,24},{9,... | collective-permute-start | bytes 884744 | tf_op jit(solution)/shard_map/ppermute | solution.py:88
  29.8 14.4 %collective-permute-start.5 = (bf16[32,4608]{1,0:T(8,128)(2,1)S(1)}, bf16[32,4608]{1,0:T(8,128)(2,1)S(1)}, u32[]{:S(2)}, u32[]{:S(2)}) collective-permute-start(bf16[32,4608]{1,0:T(8,128)(2,1)S(1)} %constant_dynamic-update-slice_fusion.refs_0_), channel_id=1, source_target_pairs={{0,24},{1,25},{2,26},{3,27},{4,28},{5,29},{6,30},{7,31},{8,16},{9,... | collective-permute-start | bytes 884744 | tf_op jit(solution)/shard_map/ppermute | solution.py:88
  41.1 9.9 %collective-permute-start.20 = (bf16[32,4608]{1,0:T(8,128)(2,1)S(1)}, bf16[32,4608]{1,0:T(8,128)(2,1)S(1)}, u32[]{:S(2)}, u32[]{:S(2)}) collective-permute-start(bf16[32,4608]{1,0:T(8,128)(2,1)S(1)} %constant_dynamic-update-slice_fusion.11.refs_3_), channel_id=1, source_target_pairs={{0,8},{1,9},{2,10},{3,11},{4,12},{5,13},{6,14},{7,15},{8,0},{9,1},... | collective-permute-start | bytes 884744 | tf_op jit(solution)/shard_map/ppermute | solution.py:88
  42.7 15.5 %collective-permute-start.21 = (bf16[32,4608]{1,0:T(8,128)(2,1)S(1)}, bf16[32,4608]{1,0:T(8,128)(2,1)S(1)}, u32[]{:S(2)}, u32[]{:S(2)}) collective-permute-start(bf16[32,4608]{1,0:T(8,128)(2,1)S(1)} %constant_dynamic-update-slice_fusion.11.refs_3_), channel_id=1, source_target_pairs={{0,16},{1,17},{2,18},{3,19},{4,20},{5,21},{6,22},{7,23},{8,24},{9,... | collective-permute-start | bytes 884744 | tf_op jit(solution)/shard_map/ppermute | solution.py:88
  44.2 19.5 %collective-permute-start.16 = (bf16[256,1664]{1,0:T(8,128)(2,1)S(1)}, bf16[256,1664]{1,0:T(8,128)(2,1)S(1)}, u32[]{:S(2)}, u32[]{:S(2)}) collective-permute-start(bf16[256,1664]{1,0:T(8,128)(2,1)S(1)} %constant_dynamic-update-slice_fusion.4.refs_1_), channel_id=1, source_target_pairs={{0,4},{1,5},{2,6},{3,7},{4,0},{5,1},{6,2},{7,3},{8,12},{9,13},{10,... | collective-permute-start | bytes 2555912 | tf_op jit(solution)/shard_map/ppermute | solution.py:88
  44.3 13.9 %collective-permute-start.22 = (bf16[32,4608]{1,0:T(8,128)(2,1)S(1)}, bf16[32,4608]{1,0:T(8,128)(2,1)S(1)}, u32[]{:S(2)}, u32[]{:S(2)}) collective-permute-start(bf16[32,4608]{1,0:T(8,128)(2,1)S(1)} %constant_dynamic-update-slice_fusion.11.refs_3_), channel_id=1, source_target_pairs={{0,24},{1,25},{2,26},{3,27},{4,28},{5,29},{6,30},{7,31},{8,16},{9,... | collective-permute-start | bytes 884744 | tf_op jit(solution)/shard_map/ppermute | solution.py:88
  44.8 13.9 %collective-permute-start.7 = (bf16[32,4608]{1,0:T(8,128)(2,1)S(1)}, bf16[32,4608]{1,0:T(8,128)(2,1)S(1)}, u32[]{:S(2)}, u32[]{:S(2)}) collective-permute-start(bf16[32,4608]{1,0:T(8,128)(2,1)S(1)} %collective-permute-done.3.refs_1_), channel_id=1, source_target_pairs={{0,4},{1,5},{2,6},{3,7},{4,0},{5,1},{6,2},{7,3},{8,12},{9,13},{10,... | collective-permute-start | bytes 884744 | tf_op jit(solution)/shard_map/ppermute | solution.py:88
  82.2 12.5 %collective-permute-start.31 = (bf16[128,2304]{1,0:T(8,128)(2,1)S(1)}, bf16[128,2304]{1,0:T(8,128)(2,1)S(1)}, u32[]{:S(2)}, u32[]{:S(2)}) collective-permute-start(bf16[128,2304]{1,0:T(8,128)(2,1)S(1)} %get-tuple-element.18), channel_id=1, source_target_pairs={{0,4},{1,5},{2,6},{3,7},{4,0},{5,1},{6,2},{7,3},{8,12},{9,13},{10,... | collective-permute-start | bytes 1769480 | tf_op jit(solution)/shard_map/ppermute | solution.py:88
  95.5 9.1 %collective-permute-start.33 = (bf16[32,2304]{1,0:T(8,128)(2,1)S(1)}, bf16[32,2304]{1,0:T(8,128)(2,1)S(1)}, u32[]{:S(2)}, u32[]{:S(2)}) collective-permute-start(bf16[32,2304]{1,0:T(8,128)(2,1)S(1)} %get-tuple-element.28), channel_id=1, source_target_pairs={{0,16},{1,17},{2,18},{3,19},{4,20},{5,21},{6,22},{7,23},{8,24},{9,... | collective-permute-start | bytes 442376 | tf_op jit(solution)/shard_map/ppermute | solution.py:88
  96.0 8.5 %collective-permute-start.34 = (bf16[32,2304]{1,0:T(8,128)(2,1)S(1)}, bf16[32,2304]{1,0:T(8,128)(2,1)S(1)}, u32[]{:S(2)}, u32[]{:S(2)}) collective-permute-start(bf16[32,2304]{1,0:T(8,128)(2,1)S(1)} %get-tuple-element.27), channel_id=1, source_target_pairs={{0,24},{1,25},{2,26},{3,27},{4,28},{5,29},{6,30},{7,31},{8,16},{9,... | collective-permute-start | bytes 442376 | tf_op jit(solution)/shard_map/ppermute | solution.py:88
  98.6 9.7 %collective-permute-start.28 = (bf16[32,2560]{1,0:T(8,128)(2,1)S(1)}, bf16[32,2560]{1,0:T(8,128)(2,1)S(1)}, u32[]{:S(2)}, u32[]{:S(2)}) collective-permute-start(bf16[32,2560]{1,0:T(8,128)(2,1)S(1)} %get-tuple-element.25), channel_id=1, source_target_pairs={{0,8},{1,9},{2,10},{3,11},{4,12},{5,13},{6,14},{7,15},{8,0},{9,1},... | collective-permute-start | bytes 491528 | tf_op jit(solution)/shard_map/ppermute | solution.py:88
  99.2 11.6 %collective-permute-start.29 = (bf16[32,2560]{1,0:T(8,128)(2,1)S(1)}, bf16[32,2560]{1,0:T(8,128)(2,1)S(1)}, u32[]{:S(2)}, u32[]{:S(2)}) collective-permute-start(bf16[32,2560]{1,0:T(8,128)(2,1)S(1)} %get-tuple-element.24), channel_id=1, source_target_pairs={{0,16},{1,17},{2,18},{3,19},{4,20},{5,21},{6,22},{7,23},{8,24},{9,... | collective-permute-start | bytes 491528 | tf_op jit(solution)/shard_map/ppermute | solution.py:88
  101.6 9.1 %collective-permute-start.30 = (bf16[32,2560]{1,0:T(8,128)(2,1)S(1)}, bf16[32,2560]{1,0:T(8,128)(2,1)S(1)}, u32[]{:S(2)}, u32[]{:S(2)}) collective-permute-start(bf16[32,2560]{1,0:T(8,128)(2,1)S(1)} %get-tuple-element.23), channel_id=1, source_target_pairs={{0,24},{1,25},{2,26},{3,27},{4,28},{5,29},{6,30},{7,31},{8,16},{9,... | collective-permute-start | bytes 491528 | tf_op jit(solution)/shard_map/ppermute | solution.py:88
  112.8 8.4 %collective-permute-start.36 = (bf16[8,4864]{1,0:T(8,128)(2,1)S(1)}, bf16[8,4864]{1,0:T(8,128)(2,1)S(1)}, u32[]{:S(2)}, u32[]{:S(2)}) collective-permute-start(bf16[8,4864]{1,0:T(8,128)(2,1)S(1)} %pad_maximum_fusion.3), channel_id=1, source_target_pairs={{0,2},{1,3},{2,0},{3,1},{4,6},{5,7},{6,4},{7,5},{8,10},{9,11},{10,... | collective-permute-start | bytes 233480 | tf_op jit(solution)/shard_map/ppermute | solution.py:88
  (28 other events, 205.3 us)
